TPU v7x, 32 devices: a whole 2x2x4 slice. The times are simulated.
32 devices in a mesh: dp: 4 (over z), expert: 8 (over y, x, core).
Axes of the slice: x: 2, y: 2, z: 4, core: 2. Of those that a mesh axis runs over, the one named last changes fastest.
Arguments:
- tokens: bfloat16 [2, 64, 197, 768], P(None, ('dp', 'expert')), may hold values from -6 to 6
- image_count: int32 [2, 32], P(None, ('dp', 'expert')), may hold values from 1 to 2, 48 in all within a row
- adapter_index: int32 [2, 64], P(None, ('dp', 'expert')), may hold values from 0 to 7
- expert_ids: int32 [2, 64, 197, 2], P(None, ('dp', 'expert')), may hold values from 0 to 7, as said below
- norm_gains: bfloat16 [2, 768], P(None, ('dp', 'expert')), may hold values from 0.25 to 1.75
- attention_in: bfloat16 [768, 2304], P(('dp', 'expert')), may hold values from -0.21875 to 0.21875
- attention_out: bfloat16 [768, 768], P(('dp', 'expert')), may hold values from -0.625 to 0.625
- router: bfloat16 [768, 8], P(('dp', 'expert')), may hold values from -0.14941406 to 0.14941406
- expert_in: bfloat16 [8, 768, 3072], P('expert', 'dp'), may hold values from -0.21875 to 0.21875
- expert_out: bfloat16 [8, 3072, 768], P('expert', 'dp'), may hold values from -0.109375 to 0.109375
- attention_down: bfloat16 [768, 4, 8, 16], P(('dp', 'expert')), may hold values from -0.21875 to 0.21875
- attention_up: bfloat16 [4, 8, 16, 768], P(None, None, None, ('dp', 'expert')), may hold values from -0.75 to 0.75
- expert_down_in: bfloat16 [8, 768, 8, 16], P('expert', 'dp'), may hold values from -0.21875 to 0.21875
- expert_up_in: bfloat16 [8, 8, 16, 3072], P('expert', None, None, 'dp'), may hold values from -0.75 to 0.75
- expert_down_out: bfloat16 [8, 3072, 8, 16], P('expert', 'dp'), may hold values from -0.15625 to 0.15625
- expert_up_out: bfloat16 [8, 8, 16, 768], P('expert', None, None, 'dp'), may hold values from -0.75 to 0.75
- cotangent: bfloat16 [2, 64, 197, 768], P(None, ('dp', 'expert')), may hold values from -6 to 6
Outputs:
- output: bfloat16 [2, 64, 197, 768], P(None, ('dp', 'expert'))
- input_grad: bfloat16 [2, 64, 197, 768], P(None, ('dp', 'expert'))
- attention_down_grad: float32 [768, 4, 8, 16], P(('dp', 'expert'))
- attention_up_grad: float32 [4, 8, 16, 768], P(None, None, None, ('dp', 'expert'))
- expert_down_in_grad: float32 [8, 768, 8, 16], P('expert', 'dp')
- expert_up_in_grad: float32 [8, 8, 16, 3072], P('expert', None, None, 'dp')
- expert_down_out_grad: float32 [8, 3072, 8, 16], P('expert', 'dp')
- expert_up_out_grad: float32 [8, 8, 16, 768], P('expert', None, None, 'dp')
Inputs may be any that keep to these rules, and one draw needn't show every extreme that they name: The first image_count[m, d] of the 2 image slots of device d in micro-batch m are live; each micro-batch's counts sum to 48. `expert_ids`: the two experts of a token differ. Among the 394 tokens of one device in one micro-batch (its 2 consecutive image slots), live or not, no expert is named more than 110 times, and in every such block some expert is named exactly 110 times.
All inputs are finite; a program needn't handle non-finite values.
Results may differ from a plain program's by a relative error of at most 0.017.
Values may be sent and summed in bfloat16 or wider, within the bound.
No kernel may reach another device: no remote copies, remote signals or barrier semaphores. Data moves between devices by JAX's collectives and lax.ppermute only.
A program may use at most 256 MiB of HBM per device.

v0:
```python
import math

import jax
import jax.numpy as jnp
from jax import lax
from jax.sharding import PartitionSpec as P

HEAD_DIM = 64
RANK = 16
ADAPTERS = 8


EPSILON = 1e-06
HIGHEST = lax.Precision.HIGHEST


def matmul(left, right):
    return jnp.dot(left, right, preferred_element_type=jnp.float32)


def times_transposed(left, right):
    return lax.dot_general(
        left, right, (((1,), (1,)), ((), ())), preferred_element_type=jnp.float32
    )


def transposed_times(left, right):
    return lax.dot_general(
        left, right, (((0,), (0,)), ((), ())), preferred_element_type=jnp.float32
    )


def layer_norm(inputs, scale_row):
    average = jnp.mean(inputs, axis=-1, keepdims=True)
    centred = inputs - average
    spread = jnp.mean(centred * centred, axis=-1, keepdims=True)
    inverse = lax.rsqrt(spread + EPSILON)
    normal = centred * inverse
    return (normal * scale_row, normal, inverse)


def norm_backward(grad_norm, normal, inverse, scale_row):
    scaled = grad_norm * scale_row
    first = jnp.mean(scaled, axis=-1, keepdims=True)
    second = jnp.mean(scaled * normal, axis=-1, keepdims=True)
    return inverse * (scaled - first - normal * second)


def gelu_exact(inputs):
    return jax.nn.gelu(inputs, approximate=False)


def adapter_select(owners):
    columns = jnp.arange(ADAPTERS * RANK, dtype=jnp.int32) // RANK
    return (owners[:, None] == columns[None, :]).astype(jnp.float32)


def route_slots(picks, experts, capacity):
    flat_picks = picks.reshape(-1)
    hits = (flat_picks[:, None] == jnp.arange(experts, dtype=jnp.int32)[None, :]).astype(jnp.int32)
    placed = jnp.sum((jnp.cumsum(hits, axis=0) - 1) * hits, axis=1)
    return flat_picks * capacity + placed


def expert_forward(weights, pair):
    inner_in, inner_out, down_in, up_in, down_out, up_out = weights
    received, received_adapt = pair
    sources, items, width = received.shape
    rows_in = received.reshape(sources * items, width)
    select = adapter_select(received_adapt.reshape(-1).astype(jnp.int32))
    thin_in = (matmul(rows_in, down_in) * select).astype(jnp.bfloat16)
    lifted = matmul(rows_in, inner_in) + matmul(thin_in, up_in)
    active = gelu_exact(lifted).astype(jnp.bfloat16)
    thin_out = (matmul(active, down_out) * select).astype(jnp.bfloat16)
    result = (matmul(active, inner_out) + matmul(thin_out, up_out)).astype(jnp.bfloat16)
    return (
        result.reshape(sources, items, width),
        lifted.reshape(sources, items, -1),
        received,
        received_adapt,
    )


def expert_backward(weights, received, received_adapt, lifted, arrived):
    inner_in, inner_out, down_in, up_in, down_out, up_out = weights
    sources, items, width = received.shape
    total_rows = sources * items
    rows_in = received.reshape(total_rows, width)
    lifted_rows = lifted.reshape(total_rows, -1)
    grad_result = arrived.reshape(total_rows, width)
    select = adapter_select(received_adapt.reshape(-1).astype(jnp.int32))
    thin_in = (matmul(rows_in, down_in) * select).astype(jnp.bfloat16)
    active, gelu_pull = jax.vjp(gelu_exact, lifted_rows)
    active = active.astype(jnp.bfloat16)
    thin_out = (matmul(active, down_out) * select).astype(jnp.bfloat16)
    grad_thin_out = (times_transposed(grad_result, up_out) * select).astype(jnp.bfloat16)
    grad_active = times_transposed(grad_result, inner_out) + times_transposed(
        grad_thin_out, down_out
    )
    grad_lifted = gelu_pull(grad_active)[0].astype(jnp.bfloat16)
    grad_thin_in = (times_transposed(grad_lifted, up_in) * select).astype(jnp.bfloat16)
    grad_received = (
        times_transposed(grad_lifted, inner_in) + times_transposed(grad_thin_in, down_in)
    ).astype(jnp.bfloat16)
    grads = (
        transposed_times(rows_in, grad_thin_in),
        transposed_times(thin_in, grad_lifted),
        transposed_times(active, grad_thin_out),
        transposed_times(thin_out, grad_result),
    )
    return (grad_received.reshape(sources, items, width), grads)


def capacity_of(rows, experts):
    return 2 * max(1, 9 * rows // (8 * experts))


def forward_micro(dense, expert_side, inputs, adapt, count, routes):
    gains, attend_in, attend_out, router_full, down_full, up_full = dense
    images, length, width = inputs.shape
    heads = width // HEAD_DIM
    rows = images * length
    narrow_width = ADAPTERS * RANK
    experts = router_full.shape[1]
    capacity = capacity_of(rows, experts)
    factor = 1.0 / math.sqrt(HEAD_DIM)
    source = inputs.astype(jnp.float32).reshape(rows, width)
    first_norm, first_normal, first_inverse = layer_norm(source, gains[0])
    normed = first_norm.astype(jnp.bfloat16)
    row_adapt = jnp.repeat(adapt, length)
    select = adapter_select(row_adapt)
    select_three = jnp.tile(select, (1, 3))
    narrow = (matmul(normed, down_full[:, : 3 * narrow_width]) * select_three).astype(jnp.bfloat16)
    widened = jnp.concatenate(
        [
            matmul(narrow[:, part * narrow_width : (part + 1) * narrow_width], up_full[part])
            for part in range(3)
        ],
        axis=1,
    )
    projected = (matmul(normed, attend_in) + widened).astype(jnp.bfloat16)
    queries, keys, values = [
        projected[:, part * width : (part + 1) * width].reshape(images, length, heads, HEAD_DIM)
        for part in range(3)
    ]
    scores = (
        jnp.einsum("ishc,ithc->ihst", queries, keys, preferred_element_type=jnp.float32) * factor
    )
    peak = jnp.max(scores, axis=-1, keepdims=True)
    exponent = jnp.exp(scores - peak)
    total = jnp.sum(exponent, axis=-1, keepdims=True)
    weights = (exponent / total).astype(jnp.bfloat16)
    log_total = peak + jnp.log(total)
    mixed = (
        jnp.einsum("ihst,ithc->ishc", weights, values, preferred_element_type=jnp.float32)
        .reshape(rows, width)
        .astype(jnp.bfloat16)
    )
    narrow_out = (matmul(mixed, down_full[:, 3 * narrow_width :]) * select).astype(jnp.bfloat16)
    hidden = source + (matmul(mixed, attend_out) + matmul(narrow_out, up_full[3]))
    second_norm, second_normal, second_inverse = layer_norm(hidden, gains[1])
    flat = second_norm.astype(jnp.bfloat16)
    picks = routes.reshape(rows, 2)
    logits = matmul(flat, router_full)
    gates = jax.nn.softmax(jnp.take_along_axis(logits, picks, axis=1), axis=-1)
    slots = route_slots(picks, experts, capacity)
    owners = jnp.arange(2 * rows, dtype=jnp.int32) // 2
    send_rows = (
        jnp.zeros((experts * capacity, width), jnp.bfloat16)
        .at[slots]
        .set(flat[owners])
        .reshape(experts, capacity, width)
    )
    send_adapt = (
        jnp.zeros((experts * capacity,), jnp.bfloat16)
        .at[slots]
        .set(row_adapt[owners].astype(jnp.bfloat16))
        .reshape(experts, capacity)
    )
    result, lifted, received, received_adapt = expert_forward(
        expert_side,
        (
            lax.all_to_all(send_rows, "expert", split_axis=0, concat_axis=0, tiled=True),
            lax.all_to_all(send_adapt, "expert", split_axis=0, concat_axis=0, tiled=True),
        ),
    )
    home = lax.all_to_all(result, "expert", split_axis=0, concat_axis=0, tiled=True)
    returned = (
        home.reshape(experts * capacity, width)[slots].astype(jnp.float32).reshape(rows, 2, width)
    )
    living = jnp.repeat((jnp.arange(images, dtype=jnp.int32) < count).astype(jnp.float32), length)[
        :, None
    ]
    output = ((hidden + jnp.sum(gates[:, :, None] * returned, axis=1)) * living).astype(
        jnp.bfloat16
    )
    kept = (
        first_normal,
        first_inverse,
        normed,
        select,
        select_three,
        narrow,
        queries,
        keys,
        values,
        log_total,
        mixed,
        narrow_out,
        second_normal,
        second_inverse,
        picks,
        gates,
        slots,
        returned,
        living,
        received,
        received_adapt,
        lifted,
    )
    return (output.reshape(images, length, width), kept)


def backward_micro(dense, expert_side, kept, cotangent_part):
    (
        first_normal,
        first_inverse,
        normed,
        select,
        select_three,
        narrow,
        queries,
        keys,
        values,
        log_total,
        mixed,
        narrow_out,
        second_normal,
        second_inverse,
        picks,
        gates,
        slots,
        returned,
        living,
        received,
        received_adapt,
        lifted,
    ) = kept
    gains, attend_in, attend_out, router_full, down_full, up_full = dense
    images, length, width = cotangent_part.shape
    heads = width // HEAD_DIM
    rows = images * length
    narrow_width = ADAPTERS * RANK
    experts = router_full.shape[1]
    capacity = capacity_of(rows, experts)
    factor = 1.0 / math.sqrt(HEAD_DIM)
    delta = cotangent_part.astype(jnp.float32).reshape(rows, width) * living
    grad_rows = (
        (gates[:, :, None] * delta[:, None, :]).astype(jnp.bfloat16).reshape(2 * rows, width)
    )
    grad_gates = jnp.sum(returned * delta[:, None, :], axis=-1)
    grad_picked = gates * (grad_gates - jnp.sum(gates * grad_gates, axis=-1, keepdims=True))
    picked_hot = (picks[:, :, None] == jnp.arange(experts, dtype=jnp.int32)[None, None, :]).astype(
        jnp.float32
    )
    grad_logits = jnp.sum(grad_picked[:, :, None] * picked_hot, axis=1)
    send_grads = (
        jnp.zeros((experts * capacity, width), jnp.bfloat16)
        .at[slots]
        .set(grad_rows)
        .reshape(experts, capacity, width)
    )
    arrived = lax.all_to_all(send_grads, "expert", split_axis=0, concat_axis=0, tiled=True)
    grad_received, expert_grads = expert_backward(
        expert_side, received, received_adapt, lifted, arrived
    )
    back_home = lax.all_to_all(grad_received, "expert", split_axis=0, concat_axis=0, tiled=True)
    grad_flat = jnp.sum(
        back_home.reshape(experts * capacity, width)[slots]
        .astype(jnp.float32)
        .reshape(rows, 2, width),
        axis=1,
    )
    grad_flat = grad_flat + jnp.dot(
        grad_logits, router_full.astype(jnp.float32).T, precision=HIGHEST
    )
    grad_hidden = delta + norm_backward(grad_flat, second_normal, second_inverse, gains[1])
    grad_branch = grad_hidden.astype(jnp.bfloat16)
    grad_narrow_out = (times_transposed(grad_branch, up_full[3]) * select).astype(jnp.bfloat16)
    grad_mixed = (
        times_transposed(grad_branch, attend_out)
        + times_transposed(grad_narrow_out, down_full[:, 3 * narrow_width :])
    ).astype(jnp.bfloat16)
    grad_heads = grad_mixed.reshape(images, length, heads, HEAD_DIM)
    scores = (
        jnp.einsum("ishc,ithc->ihst", queries, keys, preferred_element_type=jnp.float32) * factor
    )
    probs = jnp.exp(scores - log_total)
    weights = probs.astype(jnp.bfloat16)
    grad_values = jnp.einsum(
        "ihst,ishc->ithc", weights, grad_heads, preferred_element_type=jnp.float32
    )
    grad_weights = jnp.einsum(
        "ishc,ithc->ihst", grad_heads, values, preferred_element_type=jnp.float32
    )
    grad_scores = (
        probs * (grad_weights - jnp.sum(probs * grad_weights, axis=-1, keepdims=True))
    ).astype(jnp.bfloat16)
    grad_queries = (
        jnp.einsum("ihst,ithc->ishc", grad_scores, keys, preferred_element_type=jnp.float32)
        * factor
    )
    grad_keys = (
        jnp.einsum("ihst,ishc->ithc", grad_scores, queries, preferred_element_type=jnp.float32)
        * factor
    )
    grad_projected = jnp.concatenate(
        [
            grad_queries.reshape(rows, width),
            grad_keys.reshape(rows, width),
            grad_values.reshape(rows, width),
        ],
        axis=1,
    ).astype(jnp.bfloat16)
    grad_narrow = jnp.concatenate(
        [
            times_transposed(grad_projected[:, part * width : (part + 1) * width], up_full[part])
            for part in range(3)
        ],
        axis=1,
    )
    grad_narrow = (grad_narrow * select_three).astype(jnp.bfloat16)
    grad_normed = times_transposed(grad_projected, attend_in) + times_transposed(
        grad_narrow, down_full[:, : 3 * narrow_width]
    )
    grad_input = grad_hidden + norm_backward(grad_normed, first_normal, first_inverse, gains[0])
    down_grad = jnp.concatenate(
        [transposed_times(normed, grad_narrow), transposed_times(mixed, grad_narrow_out)], axis=1
    )
    up_parts = [
        transposed_times(
            narrow[:, part * narrow_width : (part + 1) * narrow_width],
            grad_projected[:, part * width : (part + 1) * width],
        )
        for part in range(3)
    ]
    up_grad = jnp.stack(up_parts + [transposed_times(narrow_out, grad_branch)], axis=0)
    new_grads = (down_grad, up_grad) + tuple(expert_grads)
    return (grad_input.astype(jnp.bfloat16).reshape(images, length, width), new_grads)


def shards(
    tokens,
    image_count,
    adapter_index,
    expert_ids,
    norm_gains,
    attention_in,
    attention_out,
    router,
    expert_in,
    expert_out,
    attention_down,
    attention_up,
    expert_down_in,
    expert_up_in,
    expert_down_out,
    expert_up_out,
    cotangent,
):
    width = tokens.shape[3]
    hidden_units = expert_in.shape[2]
    narrow_width = ADAPTERS * RANK

    def dense_fetch():
        gathered = (
            lax.all_gather(norm_gains, ("dp", "expert"), axis=1, tiled=True),
            lax.all_gather(attention_in, ("dp", "expert"), axis=0, tiled=True),
            lax.all_gather(attention_out, ("dp", "expert"), axis=0, tiled=True),
            lax.all_gather(router, ("dp", "expert"), axis=0, tiled=True),
            lax.all_gather(attention_down, ("dp", "expert"), axis=0, tiled=True),
            lax.all_gather(attention_up, ("dp", "expert"), axis=3, tiled=True),
        )
        gains, attend_in, attend_out, router_full, down_full, up_full = gathered
        return (
            gains.astype(jnp.float32),
            attend_in,
            attend_out,
            router_full,
            down_full.reshape(width, 4 * narrow_width),
            up_full.reshape(4, narrow_width, width),
        )

    def expert_fetch():
        gathered = (
            lax.all_gather(expert_in, "dp", axis=1, tiled=True),
            lax.all_gather(expert_out, "dp", axis=1, tiled=True),
            lax.all_gather(expert_down_in, "dp", axis=1, tiled=True),
            lax.all_gather(expert_up_in, "dp", axis=3, tiled=True),
            lax.all_gather(expert_down_out, "dp", axis=1, tiled=True),
            lax.all_gather(expert_up_out, "dp", axis=3, tiled=True),
        )
        inner_in, inner_out, down_in, up_in, down_out, up_out = gathered
        return (
            inner_in[0],
            inner_out[0],
            down_in[0].reshape(width, narrow_width),
            up_in[0].reshape(narrow_width, hidden_units),
            down_out[0].reshape(hidden_units, narrow_width),
            up_out[0].reshape(narrow_width, width),
        )

    def micro_step(index, carry):
        outputs, input_grads, accums = carry
        inputs = lax.dynamic_index_in_dim(tokens, index, 0, keepdims=False)
        adapt = lax.dynamic_index_in_dim(adapter_index, index, 0, keepdims=False)
        count = lax.dynamic_index_in_dim(image_count, index, 0, keepdims=False)[0]
        routes = lax.dynamic_index_in_dim(expert_ids, index, 0, keepdims=False)
        cotangent_part = lax.dynamic_index_in_dim(cotangent, index, 0, keepdims=False)
        forward_weights = (dense_fetch(), expert_fetch())
        output, kept = forward_micro(
            forward_weights[0], forward_weights[1], inputs, adapt, count, routes
        )
        backward_weights = (dense_fetch(), expert_fetch())
        grad_input, new_grads = backward_micro(
            backward_weights[0], backward_weights[1], kept, cotangent_part
        )
        accums = tuple((old + new for old, new in zip(accums, new_grads)))
        outputs = lax.dynamic_update_index_in_dim(outputs, output, index, 0)
        input_grads = lax.dynamic_update_index_in_dim(input_grads, grad_input, index, 0)
        return (outputs, input_grads, accums)

    accums = (
        jnp.zeros((width, 4 * narrow_width), jnp.float32),
        jnp.zeros((4, narrow_width, width), jnp.float32),
        jnp.zeros((width, narrow_width), jnp.float32),
        jnp.zeros((narrow_width, hidden_units), jnp.float32),
        jnp.zeros((hidden_units, narrow_width), jnp.float32),
        jnp.zeros((narrow_width, width), jnp.float32),
    )
    carry = (jnp.zeros_like(tokens), jnp.zeros_like(tokens), accums)
    outputs, input_grads, accums = lax.fori_loop(0, tokens.shape[0], micro_step, carry)
    down_total, up_total, down_in_total, up_in_total, down_out_total, up_out_total = accums
    dense_down, dense_up = (
        lax.psum_scatter(
            down_total.reshape(width, 4, ADAPTERS, RANK),
            ("dp", "expert"),
            scatter_dimension=0,
            tiled=True,
        ),
        lax.psum_scatter(
            up_total.reshape(4, ADAPTERS, RANK, width),
            ("dp", "expert"),
            scatter_dimension=3,
            tiled=True,
        ),
    )
    down_in_grad, up_in_grad, down_out_grad, up_out_grad = (
        lax.psum_scatter(
            down_in_total.reshape(1, width, ADAPTERS, RANK).astype(jnp.bfloat16),
            "dp",
            scatter_dimension=1,
            tiled=True,
        ).astype(jnp.float32),
        lax.psum_scatter(
            up_in_total.reshape(1, ADAPTERS, RANK, hidden_units).astype(jnp.bfloat16),
            "dp",
            scatter_dimension=3,
            tiled=True,
        ).astype(jnp.float32),
        lax.psum_scatter(
            down_out_total.reshape(1, hidden_units, ADAPTERS, RANK).astype(jnp.bfloat16),
            "dp",
            scatter_dimension=1,
            tiled=True,
        ).astype(jnp.float32),
        lax.psum_scatter(
            up_out_total.reshape(1, ADAPTERS, RANK, width).astype(jnp.bfloat16),
            "dp",
            scatter_dimension=3,
            tiled=True,
        ).astype(jnp.float32),
    )
    return (
        outputs,
        input_grads,
        dense_down,
        dense_up,
        down_in_grad,
        up_in_grad,
        down_out_grad,
        up_out_grad,
    )


def solution(mesh):
    return jax.shard_map(
        shards,
        mesh=mesh,
        in_specs=(
            P(None, ("dp", "expert"), None, None),
            P(None, ("dp", "expert")),
            P(None, ("dp", "expert")),
            P(None, ("dp", "expert"), None, None),
            P(None, ("dp", "expert")),
            P(("dp", "expert"), None),
            P(("dp", "expert"), None),
            P(("dp", "expert"), None),
            P("expert", "dp", None),
            P("expert", "dp", None),
            P(("dp", "expert"), None, None, None),
            P(None, None, None, ("dp", "expert")),
            P("expert", "dp", None, None),
            P("expert", None, None, "dp"),
            P("expert", "dp", None, None),
            P("expert", None, None, "dp"),
            P(None, ("dp", "expert"), None, None),
        ),
        out_specs=(
            P(None, ("dp", "expert"), None, None),
            P(None, ("dp", "expert"), None, None),
            P(("dp", "expert"), None, None, None),
            P(None, None, None, ("dp", "expert")),
            P("expert", "dp", None, None),
            P("expert", None, None, "dp"),
            P("expert", "dp", None, None),
            P("expert", None, None, "dp"),
        ),
        check_vma=False,
    )
```

profile of v0, /device:TPU:0, one launch (start us, length us, event | category | flops | bytes accessed | tf_op | source)
XLA Modules:
  0.0 1761.3 jit_solution(5166442601303363843)
XLA Ops:
  14.3 1440.7 %while.31 = (s32[]{:T(128)}, bf16[2,2,197,768]{3,1,2,0:T(2,128)(2,1)}, bf16[2,2,197,768]{3,1,2,0:T(2,128)(2,1)}, f32[768,512]{0,1:T(8,128)}, f32[4,128,768]{2,1,...) while((s32[]{:T(128)}, ...), condition=%wide.region_25.26_spmd.clone, body=%wide.region_0.25_spmd.clone.sunk | while | flops 28412825600 | bytes 801040768 | solution.py:442
  46.6 42.3 %all-gather.6 = bf16[32,24,2]{1,2,0:T(2,128)(2,1)S(1)} all-gather(bf16[1,24,2]{1,2,0:T(2,128)(2,1)S(1)} %bitcast.430), channel_id=1, replica_groups=mesh['dp'=4,'expert'=8] {'dp','expert'}, dimensions={0}, use_global_device_ids=true | all-gather | bytes 3168 | tf_op jit(solution)/shard_map/while/body/eval_jaxpr/all_gather | solution.py:377
  89.3 79.5 %all_gather.166 = bf16[768,4,8,16]{3,2,1,0:T(8,128)(2,1)} all-gather(bf16[24,4,8,16]{3,2,1,0:T(8,128)(2,1)S(1)} %get-tuple-element.1338), channel_id=1, replica_groups=mesh['dp'=4,'expert'=8] {'dp','expert'}, dimensions={0}, use_global_device_ids=true | all-gather | bytes 811008 | tf_op jit(solution)/shard_map/while/body/eval_jaxpr/all_gather | solution.py:381
  176.4 98.1 %all_gather.165 = bf16[4,8,16,768]{2,1,0,3:T(8,128)(2,1)S(1)} all-gather(bf16[4,8,16,24]{2,1,0,3:T(8,128)(2,1)S(1)} %get-tuple-element.1340), channel_id=1, replica_groups=mesh['dp'=4,'expert'=8] {'dp','expert'}, dimensions={3}, use_global_device_ids=true | all-gather | bytes 811008 | tf_op jit(solution)/shard_map/while/body/eval_jaxpr/all_gather | solution.py:382
  293.1 45.2 %all-gather.7 = bf16[32,24,8]{1,2,0:T(8,128)(2,1)S(1)} all-gather(bf16[1,24,8]{1,2,0:T(8,128)(2,1)S(1)} %bitcast.429), channel_id=1, replica_groups=mesh['dp'=4,'expert'=8] {'dp','expert'}, dimensions={0}, use_global_device_ids=true | all-gather | bytes 12672 | tf_op jit(solution)/shard_map/while/body/eval_jaxpr/all_gather | solution.py:380
  381.8 12.5 scatter_custom_fusion.18
  400.0 36.8 %all_gather.169 = bf16[1,768,8,16]{3,2,0,1:T(8,128)(2,1)S(1)} all-gather(bf16[1,192,8,16]{3,2,0,1:T(8,128)(2,1)S(1)} %copy-done.65), channel_id=1, replica_groups=mesh['dp'=4,'expert'=8] {'dp'}, dimensions={1}, use_global_device_ids=true | all-gather | bytes 245760 | tf_op jit(solution)/shard_map/while/body/eval_jaxpr/all_gather | solution.py:398
  438.3 17.7 %all_gather.170 = bf16[1,8,16,3072]{3,2,1,0:T(8,128)(2,1)} all-gather(bf16[1,8,16,768]{3,2,1,0:T(8,128)(2,1)S(1)} %copy-done.78), channel_id=1, replica_groups=mesh['dp'=4,'expert'=8] {'dp'}, dimensions={3}, use_global_device_ids=true | all-gather | bytes 983040 | tf_op jit(solution)/shard_map/while/body/eval_jaxpr/all_gather | solution.py:399
  465.8 8.7 scatter_custom_fusion.20
  481.4 30.4 %all_gather.172 = bf16[1,8,16,768]{2,1,0,3:T(8,128)(2,1)S(1)} all-gather(bf16[1,8,16,192]{2,1,0,3:T(8,128)(2,1)} %get-tuple-element.1349), channel_id=1, replica_groups=mesh['dp'=4,'expert'=8] {'dp'}, dimensions={3}, use_global_device_ids=true | all-gather | bytes 245760 | tf_op jit(solution)/shard_map/while/body/eval_jaxpr/all_gather | solution.py:401
  514.8 18.7 %all_gather.173 = bf16[1,3072,8,16]{1,3,2,0:T(8,128)(2,1)} all-gather(bf16[1,768,8,16]{1,3,2,0:T(8,128)(2,1)} %get-tuple-element.1348), channel_id=1, replica_groups=mesh['dp'=4,'expert'=8] {'dp'}, dimensions={1}, use_global_device_ids=true | all-gather | bytes 983040 | tf_op jit(solution)/shard_map/while/body/eval_jaxpr/all_gather | solution.py:400
  548.3 27.2 %multiply_convert_fusion.23 = (bf16[880,3072]{1,0:T(8,128)(2,1)S(1)}, f32[880,3072]{1,0:T(8,128)}, f32[880,3072]{1,0:T(8,128)}) fusion(f32[880,3072]{1,0:T(8,128)S(1)} %fusion.413, bf16[880,128]{1,0:T(8,128)(2,1)S(1)} %copy-done.74, bf16[128,3072]{1,0:T(8,128)(2,1)S(1)} %bitcast.412), kind=kOutput, calls=%fused_computation.11.clone.1 | convolution fusion | flops 870481920 | bytes 38858752 | tf_op jit(solution)/shard_map/while/body/eval_jaxpr/dot_general | solution.py:18
  593.2 9.4 fusion.418
  602.5 13.0 add_convert_fusion.8
  760.9 40.6 %all-gather.6 = bf16[32,24,2]{1,2,0:T(2,128)(2,1)S(1)} all-gather(bf16[1,24,2]{1,2,0:T(2,128)(2,1)S(1)} %bitcast.430), channel_id=1, replica_groups=mesh['dp'=4,'expert'=8] {'dp','expert'}, dimensions={0}, use_global_device_ids=true | all-gather | bytes 3168 | tf_op jit(solution)/shard_map/while/body/eval_jaxpr/all_gather | solution.py:377
  801.8 80.9 %all_gather.166 = bf16[768,4,8,16]{3,2,1,0:T(8,128)(2,1)} all-gather(bf16[24,4,8,16]{3,2,1,0:T(8,128)(2,1)S(1)} %get-tuple-element.1338), channel_id=1, replica_groups=mesh['dp'=4,'expert'=8] {'dp','expert'}, dimensions={0}, use_global_device_ids=true | all-gather | bytes 811008 | tf_op jit(solution)/shard_map/while/body/eval_jaxpr/all_gather | solution.py:381
  890.3 97.4 %all_gather.165 = bf16[4,8,16,768]{2,1,0,3:T(8,128)(2,1)S(1)} all-gather(bf16[4,8,16,24]{2,1,0,3:T(8,128)(2,1)S(1)} %get-tuple-element.1340), channel_id=1, replica_groups=mesh['dp'=4,'expert'=8] {'dp','expert'}, dimensions={3}, use_global_device_ids=true | all-gather | bytes 811008 | tf_op jit(solution)/shard_map/while/body/eval_jaxpr/all_gather | solution.py:382
  1006.2 46.9 %all-gather.7 = bf16[32,24,8]{1,2,0:T(8,128)(2,1)S(1)} all-gather(bf16[1,24,8]{1,2,0:T(8,128)(2,1)S(1)} %bitcast.429), channel_id=1, replica_groups=mesh['dp'=4,'expert'=8] {'dp','expert'}, dimensions={0}, use_global_device_ids=true | all-gather | bytes 12672 | tf_op jit(solution)/shard_map/while/body/eval_jaxpr/all_gather | solution.py:380
  1096.6 12.7 scatter_custom_fusion.18
  1115.1 38.6 %all_gather.169 = bf16[1,768,8,16]{3,2,0,1:T(8,128)(2,1)S(1)} all-gather(bf16[1,192,8,16]{3,2,0,1:T(8,128)(2,1)S(1)} %copy-done.65), channel_id=1, replica_groups=mesh['dp'=4,'expert'=8] {'dp'}, dimensions={1}, use_global_device_ids=true | all-gather | bytes 245760 | tf_op jit(solution)/shard_map/while/body/eval_jaxpr/all_gather | solution.py:398
  1155.2 17.7 %all_gather.170 = bf16[1,8,16,3072]{3,2,1,0:T(8,128)(2,1)} all-gather(bf16[1,8,16,768]{3,2,1,0:T(8,128)(2,1)S(1)} %copy-done.78), channel_id=1, replica_groups=mesh['dp'=4,'expert'=8] {'dp'}, dimensions={3}, use_global_device_ids=true | all-gather | bytes 983040 | tf_op jit(solution)/shard_map/while/body/eval_jaxpr/all_gather | solution.py:399
  1198.3 30.4 %all_gather.172 = bf16[1,8,16,768]{2,1,0,3:T(8,128)(2,1)S(1)} all-gather(bf16[1,8,16,192]{2,1,0,3:T(8,128)(2,1)} %get-tuple-element.1349), channel_id=1, replica_groups=mesh['dp'=4,'expert'=8] {'dp'}, dimensions={3}, use_global_device_ids=true | all-gather | bytes 245760 | tf_op jit(solution)/shard_map/while/body/eval_jaxpr/all_gather | solution.py:401
  1231.7 18.5 %all_gather.173 = bf16[1,3072,8,16]{1,3,2,0:T(8,128)(2,1)} all-gather(bf16[1,768,8,16]{1,3,2,0:T(8,128)(2,1)} %get-tuple-element.1348), channel_id=1, replica_groups=mesh['dp'=4,'expert'=8] {'dp'}, dimensions={1}, use_global_device_ids=true | all-gather | bytes 983040 | tf_op jit(solution)/shard_map/while/body/eval_jaxpr/all_gather | solution.py:400
  1264.9 27.2 %multiply_convert_fusion.23 = (bf16[880,3072]{1,0:T(8,128)(2,1)S(1)}, f32[880,3072]{1,0:T(8,128)}, f32[880,3072]{1,0:T(8,128)}) fusion(f32[880,3072]{1,0:T(8,128)S(1)} %fusion.413, bf16[880,128]{1,0:T(8,128)(2,1)S(1)} %copy-done.74, bf16[128,3072]{1,0:T(8,128)(2,1)S(1)} %bitcast.412), kind=kOutput, calls=%fused_computation.11.clone.1 | convolution fusion | flops 870481920 | bytes 38858752 | tf_op jit(solution)/shard_map/while/body/eval_jaxpr/dot_general | solution.py:18
  1309.8 9.4 fusion.418
  1319.2 13.0 add_convert_fusion.8
  1466.8 10.5 copy.299
  1477.3 11.6 reshape.1225
  1500.3 21.7 %reduce-scatter.17.cloned.1.call-done = bf16[1,768,8,16]{1,3,2,0:T(8,128)(2,1)} async-done(((bf16[1,3072,8,16]{1,3,2,0:T(8,128)(2,1)}), bf16[1,768,8,16]{1,3,2,0:T(8,128)(2,1)}) %reduce-scatter.17.cloned.1.call-update) | async-done | bytes 196624 | tf_op jit(solution)/shard_map/reduce_scatter | solution.py:471
  1523.7 23.3 %reduce-scatter.15.cloned.1.call-done = bf16[1,8,16,768]{3,2,1,0:T(8,128)(2,1)} async-done(((bf16[1,8,16,3072]{3,2,1,0:T(8,128)(2,1)}), bf16[1,8,16,768]{3,2,1,0:T(8,128)(2,1)}) %reduce-scatter.15.cloned.1.call-update) | async-done | bytes 196624 | tf_op jit(solution)/shard_map/reduce_scatter | solution.py:465
  1548.7 101.0 %reduce-scatter.21.cloned.1.call-done = f32[24,512]{1,0:T(8,128)} async-done(((f32[768,512]{1,0:T(8,128)}), f32[24,512]{1,0:T(8,128)}) %reduce-scatter.21.cloned.1.call-update) | async-done | bytes 49168
  1651.6 100.4 %reduce-scatter.19.cloned.1.call-done = f32[24,512]{1,0:T(8,128)} async-done(((f32[768,512]{1,0:T(8,128)}), f32[24,512]{1,0:T(8,128)}) %reduce-scatter.19.cloned.1.call-update) | async-done | bytes 49168
  (919 shorter events, 593.3 us)
Async XLA Ops:
  14.6 337.3 %all-gather.13.cloned.1.call-start = ((), (), s32[]{:S(2)}) async-start(), calls=%async_computation.17 | async-start | bytes 3649536 | tf_op jit(solution)/shard_map/while/body/eval_jaxpr/all_gather | solution.py:378
  15.3 362.6 %all-gather.15.cloned.1.call-start = ((), (), s32[]{:S(2)}) async-start(), calls=%async_computation.18 | async-start | bytes 1216512 | tf_op jit(solution)/shard_map/while/body/eval_jaxpr/all_gather | solution.py:379
  16.1 525.9 %all-gather.17.cloned.1.call-start = ((), (), s32[]{:S(2)}) async-start(), calls=%async_computation.19 | async-start | bytes 5898240 | tf_op jit(solution)/shard_map/while/body/eval_jaxpr/all_gather | solution.py:396
  17.6 358.7 %copy-start = (s32[394]{0:T(512)}, s32[394]{0:T(512)S(1)}, u32[]{:S(2)}) copy-start(s32[394]{0:T(512)S(1)} %eq.332) | copy-start | bytes 4732 | tf_op jit(solution)/shard_map/while
  36.2 359.4 %all-to-all-start.1 = ((bf16[8,1,110]{2,1,0:T(2,128)(2,1)}), bf16[8,1,110]{2,1,0:T(2,128)(2,1)S(1)}, u32[]{:S(2)}, u32[]{:S(2)}) async-start(bf16[8,1,110]{2,1,0:T(2,128)(2,1)} %all_to_all.72), calls=%async_computation.1 | async-start | bytes 8192 | tf_op jit(solution)/shard_map/while/body/eval_jaxpr/all_to_all | solution.py:184
  41.4 538.1 %all-gather.19.cloned.1.call-start = ((), (), s32[]{:S(2)}) async-start(), calls=%async_computation.20 | async-start | bytes 5898240 | tf_op jit(solution)/shard_map/while/body/eval_jaxpr/all_gather | solution.py:397
  44.4 489.5 %copy-start.90 = (s32[394,2]{0,1:T(2,128)}, s32[394,2]{0,1:T(2,128)S(1)}, u32[]{:S(2)}) copy-start(s32[394,2]{0,1:T(2,128)S(1)} %reshape.1332) | copy-start | bytes 9460 | tf_op jit(solution)/shard_map/while
  46.6 333.4 %copy-start.3 = (f32[394,768]{1,0:T(8,128)}, f32[394,768]{1,0:T(8,128)S(1)}, u32[]{:S(2)}) copy-start(f32[394,768]{1,0:T(8,128)S(1)} %reshape.1314) | copy-start | bytes 3631108 | tf_op jit(solution)/shard_map/while
  395.6 81.2 %all-to-all-start = ((bf16[8,110,768]{2,1,0:T(8,128)(2,1)}), bf16[8,110,768]{2,1,0:T(8,128)(2,1)}, u32[]{:S(2)}, u32[]{:S(2)}) async-start(bf16[8,110,768]{2,1,0:T(8,128)(2,1)} %reshape.1319), calls=%async_computation | async-start | bytes 2752512 | tf_op jit(solution)/shard_map/while/body/eval_jaxpr/all_to_all | solution.py:183
  476.8 61.3 %all-to-all-start.2 = ((bf16[8,110,768]{2,1,0:T(8,128)(2,1)}), bf16[8,110,768]{2,1,0:T(8,128)(2,1)S(1)}, u32[]{:S(2)}, u32[]{:S(2)}) async-start(bf16[8,110,768]{2,1,0:T(8,128)(2,1)} %reshape.1326), calls=%async_computation.2 | async-start | bytes 2752512 | tf_op jit(solution)/shard_map/while/body/eval_jaxpr/all_to_all | solution.py:273
  589.1 48.2 %all-to-all-start.4 = ((bf16[8,110,768]{2,1,0:T(8,128)(2,1)}), bf16[8,110,768]{2,1,0:T(8,128)(2,1)S(1)}, u32[]{:S(2)}, u32[]{:S(2)}) async-start(bf16[8,110,768]{2,1,0:T(8,128)(2,1)} %reshape.1333), calls=%async_computation.4 | async-start | bytes 2752512 | tf_op jit(solution)/shard_map/while/body/eval_jaxpr/all_to_all | solution.py:187
  637.3 23.3 %all-to-all-start.3 = ((bf16[8,110,768]{2,1,0:T(8,128)(2,1)}), bf16[8,110,768]{2,1,0:T(8,128)(2,1)}, u32[]{:S(2)}, u32[]{:S(2)}) async-start(bf16[8,110,768]{2,1,0:T(8,128)(2,1)} %reshape.1328), calls=%async_computation.3 | async-start | bytes 2752512 | tf_op jit(solution)/shard_map/while/body/eval_jaxpr/all_to_all | solution.py:277
  730.8 336.0 %all-gather.13.cloned.1.call-start = ((), (), s32[]{:S(2)}) async-start(), calls=%async_computation.17 | async-start | bytes 3649536 | tf_op jit(solution)/shard_map/while/body/eval_jaxpr/all_gather | solution.py:378
  731.4 361.4 %all-gather.15.cloned.1.call-start = ((), (), s32[]{:S(2)}) async-start(), calls=%async_computation.18 | async-start | bytes 1216512 | tf_op jit(solution)/shard_map/while/body/eval_jaxpr/all_gather | solution.py:379
  732.0 526.6 %all-gather.17.cloned.1.call-start = ((), (), s32[]{:S(2)}) async-start(), calls=%async_computation.19 | async-start | bytes 5898240 | tf_op jit(solution)/shard_map/while/body/eval_jaxpr/all_gather | solution.py:396
  733.6 357.6 %copy-start = (s32[394]{0:T(512)}, s32[394]{0:T(512)S(1)}, u32[]{:S(2)}) copy-start(s32[394]{0:T(512)S(1)} %eq.332) | copy-start | bytes 4732 | tf_op jit(solution)/shard_map/while
  752.2 358.5 %all-to-all-start.1 = ((bf16[8,1,110]{2,1,0:T(2,128)(2,1)}), bf16[8,1,110]{2,1,0:T(2,128)(2,1)S(1)}, u32[]{:S(2)}, u32[]{:S(2)}) async-start(bf16[8,1,110]{2,1,0:T(2,128)(2,1)} %all_to_all.72), calls=%async_computation.1 | async-start | bytes 8192 | tf_op jit(solution)/shard_map/while/body/eval_jaxpr/all_to_all | solution.py:184
  755.5 540.7 %all-gather.19.cloned.1.call-start = ((), (), s32[]{:S(2)}) async-start(), calls=%async_computation.20 | async-start | bytes 5898240 | tf_op jit(solution)/shard_map/while/body/eval_jaxpr/all_gather | solution.py:397
  758.3 308.4 %copy-start.94 = (f32[394]{0:T(512)}, f32[394]{0:T(512)S(1)}, u32[]{:S(2)}) copy-start(f32[394]{0:T(512)S(1)} %div.237) | copy-start | bytes 4732 | tf_op jit(solution)/shard_map/while
  758.6 491.9 %copy-start.90 = (s32[394,2]{0,1:T(2,128)}, s32[394,2]{0,1:T(2,128)S(1)}, u32[]{:S(2)}) copy-start(s32[394,2]{0,1:T(2,128)S(1)} %reshape.1332) | copy-start | bytes 9460 | tf_op jit(solution)/shard_map/while
  758.7 308.1 %copy-start.96 = (f32[394]{0:T(512)}, f32[394]{0:T(512)S(1)}, u32[]{:S(2)}) copy-start(f32[394]{0:T(512)S(1)} %rsqrt.49) | copy-start | bytes 4732 | tf_op jit(solution)/shard_map/while
  760.8 334.0 %copy-start.3 = (f32[394,768]{1,0:T(8,128)}, f32[394,768]{1,0:T(8,128)S(1)}, u32[]{:S(2)}) copy-start(f32[394,768]{1,0:T(8,128)S(1)} %reshape.1314) | copy-start | bytes 3631108 | tf_op jit(solution)/shard_map/while
  1110.7 83.0 %all-to-all-start = ((bf16[8,110,768]{2,1,0:T(8,128)(2,1)}), bf16[8,110,768]{2,1,0:T(8,128)(2,1)}, u32[]{:S(2)}, u32[]{:S(2)}) async-start(bf16[8,110,768]{2,1,0:T(8,128)(2,1)} %reshape.1319), calls=%async_computation | async-start | bytes 2752512 | tf_op jit(solution)/shard_map/while/body/eval_jaxpr/all_to_all | solution.py:183
  1193.7 61.1 %all-to-all-start.2 = ((bf16[8,110,768]{2,1,0:T(8,128)(2,1)}), bf16[8,110,768]{2,1,0:T(8,128)(2,1)S(1)}, u32[]{:S(2)}, u32[]{:S(2)}) async-start(bf16[8,110,768]{2,1,0:T(8,128)(2,1)} %reshape.1326), calls=%async_computation.2 | async-start | bytes 2752512 | tf_op jit(solution)/shard_map/while/body/eval_jaxpr/all_to_all | solution.py:273
  1305.8 49.9 %all-to-all-start.4 = ((bf16[8,110,768]{2,1,0:T(8,128)(2,1)}), bf16[8,110,768]{2,1,0:T(8,128)(2,1)S(1)}, u32[]{:S(2)}, u32[]{:S(2)}) async-start(bf16[8,110,768]{2,1,0:T(8,128)(2,1)} %reshape.1333), calls=%async_computation.4 | async-start | bytes 2752512 | tf_op jit(solution)/shard_map/while/body/eval_jaxpr/all_to_all | solution.py:187
  1355.6 23.3 %all-to-all-start.3 = ((bf16[8,110,768]{2,1,0:T(8,128)(2,1)}), bf16[8,110,768]{2,1,0:T(8,128)(2,1)}, u32[]{:S(2)}, u32[]{:S(2)}) async-start(bf16[8,110,768]{2,1,0:T(8,128)(2,1)} %reshape.1328), calls=%async_computation.3 | async-start | bytes 2752512 | tf_op jit(solution)/shard_map/while/body/eval_jaxpr/all_to_all | solution.py:277
  1455.0 37.0 %reduce-scatter.23.cloned.1.call-start = ((), (), s32[]{:S(2)}) async-start(), calls=%async_computation.15 | async-start | bytes 245760
  1459.0 39.3 %reduce-scatter.25.cloned.1.call-start = ((), (), s32[]{:S(2)}) async-start(), calls=%async_computation.16 | async-start | bytes 245760
  1461.9 60.1 %reduce-scatter.17.cloned.1.call-start = ((), (), s32[]{:S(2)}) async-start(), calls=%async_computation.12 | async-start | bytes 983040 | tf_op jit(solution)/shard_map/reduce_scatter | solution.py:471
  1464.6 82.4 %reduce-scatter.15.cloned.1.call-start = ((), (), s32[]{:S(2)}) async-start(), calls=%async_computation.11 | async-start | bytes 983040 | tf_op jit(solution)/shard_map/reduce_scatter | solution.py:465
  1466.1 183.6 %reduce-scatter.21.cloned.1.call-start = ((), (), s32[]{:S(2)}) async-start(), calls=%async_computation.14 | async-start | bytes 1622016
  1488.9 263.0 %reduce-scatter.19.cloned.1.call-start = ((), (), s32[]{:S(2)}) async-start(), calls=%async_computation.13 | async-start | bytes 1622016
  (215 other events, 3306.7 us)
Sparse Core Ops, SparseCore 0:
  18.3 62.7 all-gather.12
  84.0 60.8 all-gather.14
  146.4 115.1 all-gather.16
  263.1 96.6 all-gather.18
  734.2 58.0 all-gather.12
  795.0 60.2 all-gather.14
  856.9 112.5 all-gather.16
  971.0 98.8 all-gather.18
Sparse Core Ops, SparseCore 1:
  1459.1 18.6 reduce-scatter.22
  1480.4 17.8 reduce-scatter.24
  1500.5 21.5 reduce-scatter.16
  1524.3 22.6 reduce-scatter.14
  1552.3 97.4 reduce-scatter.20
  1655.0 97.0 reduce-scatter.18
where the time goes:
time: 1770 us; the launch traced here: 1760 us
  blocking collectives  740 us (42%)
  local copies, waits for them, and re-layouts  347 us (20%)
  matrix products  268 us (15%)
  waiting for transfers between devices  259 us (15%)
  other arithmetic  77.1 us (4%)
  starting transfers between devices  44 us (2%)
    unnamed x10, waiting for transfers between devices  206 us
    all_gather x2, blocking collectives, dense_fetch(): lax.all_gather(attention_up, ('dp', 'expert'), axis=3, tiled=True)  195 us
    all_gather x2, blocking collectives, dense_fetch(): lax.all_gather(attention_down, ('dp', 'expert'), axis=0, tiled=True)  160 us
    dot_general x30, matrix products, matmul(): return jnp.dot(left, right, preferred_element_type=jnp.float32)  119 us
    all_gather x2, blocking collectives, dense_fetch(): lax.all_gather(router, ('dp', 'expert'), axis=0, tiled=True)  92.2 us
    dot_general x28, matrix products, times_transposed(): lax.dot_general(left, right, (((1,), (1,)), ((), ())), preferred_element_...  87.1 us
    all_gather x2, blocking collectives, dense_fetch(): lax.all_gather(norm_gains, ('dp', 'expert'), axis=1, tiled=True)  82.9 us
    all_gather x2, blocking collectives, expert_fetch(): lax.all_gather(expert_down_in, 'dp', axis=1, tiled=True)  75.4 us
  transfers between devices with their start and end apart: 24, of which 7 were waited for; matrix products, arithmetic and copies ran while one was open for 29% of the time, Pallas kernels for 0%

commit v1 on v0

v1 whole, which is shorter than its diff:
```python
import functools
import math

import jax
import jax.numpy as jnp
from jax import lax
from jax.experimental import pallas as pl
from jax.experimental.pallas import tpu as pltpu
from jax.sharding import PartitionSpec as P

HEAD_DIM = 64
RANK = 16
ADAPTERS = 8
NARROW = ADAPTERS * RANK
LANES = 128
EPSILON = 1e-06
BF16 = jnp.bfloat16
F32 = jnp.float32
VMEM_LIMIT = 60 * 1024 * 1024


def mm(left, right):
    return lax.dot_general(left, right, (((1,), (0,)), ((), ())), preferred_element_type=F32)


def mm_nt(left, right):
    return lax.dot_general(left, right, (((1,), (1,)), ((), ())), preferred_element_type=F32)


def mm_tn(left, right):
    return lax.dot_general(left, right, (((0,), (0,)), ((), ())), preferred_element_type=F32)


def normal_of(value):
    average = jnp.mean(value, axis=-1, keepdims=True)
    centred = value - average
    spread = jnp.mean(centred * centred, axis=-1, keepdims=True)
    inverse = lax.rsqrt(spread + EPSILON)
    return centred * inverse, inverse


def norm_back(grad_norm, normal, inverse, scale_row):
    scaled = grad_norm * scale_row
    first = jnp.mean(scaled, axis=-1, keepdims=True)
    second = jnp.mean(scaled * normal, axis=-1, keepdims=True)
    return inverse * (scaled - first - normal * second)


def capacity_of(rows, experts):
    return 2 * max(1, 9 * rows // (8 * experts))


def lane_adapter(shape):
    return lax.broadcasted_iota(jnp.int32, shape, len(shape) - 1) % NARROW // RANK


def attention_forward_kernel(
    adapt_ref, x_ref, a_ref, b_ref, gains_ref, slots_ref,
    qkv_ref, weights_ref, mixed_ref, narrow_ref, hidden_ref, send_ref,
):
    step = pl.program_id(0)
    width = x_ref.shape[2]
    heads = width // HEAD_DIM
    x = x_ref[0].astype(F32)
    length = x.shape[0]
    normal, _ = normal_of(x)
    normed = (normal * gains_ref[0:1, :]).astype(BF16)
    adapter = adapt_ref[step]
    down_at = 2 * width
    mask = (lane_adapter((1, 3 * NARROW)) == adapter).astype(F32)
    narrow = (mm(normed, a_ref[:, down_at : down_at + 3 * NARROW]) * mask).astype(BF16)
    narrow_ref[0, :, : 3 * NARROW] = narrow
    for part in range(3):
        matrix = (a_ref[:, :width], a_ref[:, width : 2 * width], b_ref[:, :width])[part]
        up_at = 2 * width + part * NARROW
        block = mm(normed, matrix) + mm_nt(
            narrow[:, part * NARROW : (part + 1) * NARROW], b_ref[:, up_at : up_at + NARROW]
        )
        qkv_ref[0, :, part * width : (part + 1) * width] = block.astype(BF16)
    low_half = lax.broadcasted_iota(jnp.int32, (length, LANES), 1) < HEAD_DIM
    factor = 1.0 / math.sqrt(HEAD_DIM)
    for pair in range(heads // 2):
        at = pair * LANES
        queries = qkv_ref[0, :, at : at + LANES]
        keys = qkv_ref[0, :, width + at : width + at + LANES]
        values = qkv_ref[0, :, 2 * width + at : 2 * width + at + LANES]
        halves = []
        for half in range(2):
            own = low_half if half == 0 else jnp.logical_not(low_half)
            masked = jnp.where(own, queries, jnp.zeros_like(queries))
            scores = mm_nt(masked, keys) * factor
            peak = jnp.max(scores, axis=-1, keepdims=True)
            exponent = jnp.exp(scores - peak)
            total = jnp.sum(exponent, axis=-1, keepdims=True)
            weights = (exponent * (1.0 / total)).astype(BF16)
            weights_ref[0, 2 * pair + half] = weights
            halves.append(mm(weights, values))
        mixed_ref[0, :, at : at + LANES] = jnp.where(low_half, halves[0], halves[1]).astype(BF16)
    mixed = mixed_ref[0]
    out_mask = mask[:, :NARROW]
    narrow_out = (mm(mixed, a_ref[:, down_at + 3 * NARROW : down_at + 4 * NARROW]) * out_mask).astype(BF16)
    narrow_ref[0, :, 3 * NARROW :] = narrow_out
    up_at = 2 * width + 3 * NARROW
    hidden = x + (mm(mixed, b_ref[:, width : 2 * width]) + mm_nt(narrow_out, b_ref[:, up_at : up_at + NARROW]))
    hidden_ref[0] = hidden
    second, _ = normal_of(hidden)
    flat = (second * gains_ref[1:2, :]).astype(BF16)
    slot_ids = lax.broadcasted_iota(jnp.int32, (send_ref.shape[0] * send_ref.shape[1], length), 0)
    hit = jnp.logical_or(slot_ids == slots_ref[0, 0:1, :], slot_ids == slots_ref[0, 1:2, :])
    sent = mm(hit.astype(F32).astype(BF16), flat).astype(BF16).reshape(send_ref.shape)

    @pl.when(step == 0)
    def _():
        send_ref[...] = sent

    @pl.when(step > 0)
    def _():
        send_ref[...] = send_ref[...] + sent


def attention_forward(micro, adapt, x4, side_a, side_b, gains, slots_row, experts, padded):
    images = adapt.shape[0]
    _, length, width = x4.shape
    heads = width // HEAD_DIM
    first = micro * images
    whole = lambda array: pl.BlockSpec(array.shape, lambda i, *_: (0,) * array.ndim)
    image = lambda *dims: pl.BlockSpec((1,) + dims, lambda i, *_: (i,) + (0,) * len(dims))
    return pl.pallas_call(
        attention_forward_kernel,
        grid_spec=pltpu.PrefetchScalarGridSpec(
            num_scalar_prefetch=1,
            grid=(images,),
            in_specs=[
                pl.BlockSpec((1, length, width), lambda i, *_: (first + i, 0, 0)),
                whole(side_a),
                whole(side_b),
                whole(gains),
                pl.BlockSpec((1, 2, length), lambda i, *_: (first + i, 0, 0)),
            ],
            out_specs=[
                image(length, 3 * width),
                image(heads, length, length),
                image(length, width),
                image(length, 4 * NARROW),
                image(length, width),
                pl.BlockSpec((experts, padded, width), lambda i, *_: (0, 0, 0)),
            ],
        ),
        out_shape=[
            jax.ShapeDtypeStruct((images, length, 3 * width), BF16),
            jax.ShapeDtypeStruct((images, heads, length, length), BF16),
            jax.ShapeDtypeStruct((images, length, width), BF16),
            jax.ShapeDtypeStruct((images, length, 4 * NARROW), BF16),
            jax.ShapeDtypeStruct((images, length, width), F32),
            jax.ShapeDtypeStruct((experts, padded, width), BF16),
        ],
        compiler_params=pltpu.CompilerParams(vmem_limit_bytes=VMEM_LIMIT),
        name="attention_forward",
    )(adapt, x4, side_a, side_b, gains, slots_row)


def attention_backward_kernel(
    adapt_ref, count_ref, x_ref, cot_ref, a_ref, b_ref, gains_ref, slots_ref,
    qkv_ref, weights_ref, mixed_ref, narrow_ref, hidden_ref, home_ref,
    grad_ref, down_grad_ref, up_grad_ref, grad_qkv_ref, grad_mixed_ref,
):
    step = pl.program_id(0)
    width = x_ref.shape[2]
    heads = width // HEAD_DIM
    x = x_ref[0].astype(F32)
    length = x.shape[0]
    adapter = adapt_ref[step]
    live = jnp.where(step < count_ref[0], 1.0, 0.0).astype(F32)
    factor = 1.0 / math.sqrt(HEAD_DIM)
    mask = (lane_adapter((1, 3 * NARROW)) == adapter).astype(F32)
    out_mask = mask[:, :NARROW]
    down_at = 2 * width

    delta = cot_ref[0].astype(F32) * live
    slots = home_ref.shape[0] * home_ref.shape[1]
    slot_ids = lax.broadcasted_iota(jnp.int32, (length, slots), 1)
    hit = jnp.logical_or(slot_ids == slots_ref[0, :, 0:1], slot_ids == slots_ref[0, :, 1:2])
    grad_flat = mm(hit.astype(F32).astype(BF16), home_ref[...].reshape(slots, width))
    second, second_inverse = normal_of(hidden_ref[0])
    grad_hidden = delta + norm_back(grad_flat, second, second_inverse, gains_ref[1:2, :])
    branch = grad_hidden.astype(BF16)
    up_at = 2 * width + 3 * NARROW
    grad_narrow_out = (mm(branch, b_ref[:, up_at : up_at + NARROW]) * out_mask).astype(BF16)
    grad_mixed_ref[...] = (
        mm_nt(branch, b_ref[:, width : 2 * width])
        + mm_nt(grad_narrow_out, a_ref[:, down_at + 3 * NARROW : down_at + 4 * NARROW])
    ).astype(BF16)
    low_half = lax.broadcasted_iota(jnp.int32, (length, LANES), 1) < HEAD_DIM
    for pair in range(heads // 2):
        at = pair * LANES
        queries = qkv_ref[0, :, at : at + LANES]
        keys = qkv_ref[0, :, width + at : width + at + LANES]
        values = qkv_ref[0, :, 2 * width + at : 2 * width + at + LANES]
        mixed_grad = grad_mixed_ref[:, at : at + LANES]
        parts = []
        for half in range(2):
            own = low_half if half == 0 else jnp.logical_not(low_half)
            masked = jnp.where(own, mixed_grad, jnp.zeros_like(mixed_grad))
            weights = weights_ref[0, 2 * pair + half]
            probs = weights.astype(F32)
            grad_probs = mm_nt(masked, values)
            inner = jnp.sum(probs * grad_probs, axis=-1, keepdims=True)
            grad_scores = (probs * (grad_probs - inner)).astype(BF16)
            parts.append(
                (mm(grad_scores, keys), mm_tn(grad_scores, queries), mm_tn(weights, mixed_grad))
            )
        for part in range(3):
            merged = jnp.where(low_half, parts[0][part], parts[1][part])
            if part < 2:
                merged = merged * factor
            grad_qkv_ref[:, part * width + at : part * width + at + LANES] = merged.astype(BF16)
    normal, inverse = normal_of(x)
    normed = (normal * gains_ref[0:1, :]).astype(BF16)
    mixed = mixed_ref[0]
    grad_normed = None
    for part in range(3):
        block = grad_qkv_ref[:, part * width : (part + 1) * width]
        matrix = (a_ref[:, :width], a_ref[:, width : 2 * width], b_ref[:, :width])[part]
        up_at = 2 * width + part * NARROW
        narrow_mask = mask[:, :NARROW]
        grad_narrow = (mm(block, b_ref[:, up_at : up_at + NARROW]) * narrow_mask).astype(BF16)
        down_part = down_at + part * NARROW
        term = mm_nt(block, matrix) + mm_nt(grad_narrow, a_ref[:, down_part : down_part + NARROW])
        grad_normed = term if grad_normed is None else grad_normed + term
        down_new = mm_tn(normed, grad_narrow)
        up_new = mm_tn(block, narrow_ref[0, :, part * NARROW : (part + 1) * NARROW])
        cols = slice(part * NARROW, (part + 1) * NARROW)

        @pl.when(step == 0)
        def _(cols=cols, down_new=down_new, up_new=up_new):
            down_grad_ref[:, cols] = down_new
            up_grad_ref[:, cols] = up_new

        @pl.when(step > 0)
        def _(cols=cols, down_new=down_new, up_new=up_new):
            down_grad_ref[:, cols] = down_grad_ref[:, cols] + down_new
            up_grad_ref[:, cols] = up_grad_ref[:, cols] + up_new

    cols = slice(3 * NARROW, 4 * NARROW)
    down_new = mm_tn(mixed, grad_narrow_out)
    up_new = mm_tn(branch, narrow_ref[0, :, 3 * NARROW :])

    @pl.when(step == 0)
    def _():
        down_grad_ref[:, cols] = down_new
        up_grad_ref[:, cols] = up_new

    @pl.when(step > 0)
    def _():
        down_grad_ref[:, cols] = down_grad_ref[:, cols] + down_new
        up_grad_ref[:, cols] = up_grad_ref[:, cols] + up_new

    grad_ref[0] = (grad_hidden + norm_back(grad_normed, normal, inverse, gains_ref[0:1, :])).astype(BF16)


def attention_backward(micro, adapt, count, x4, cot4, side_a, side_b, gains, slots_col, kept, home):
    qkv, weights, mixed, narrow, hidden = kept
    images = adapt.shape[0]
    _, length, width = x4.shape
    heads = width // HEAD_DIM
    first = micro * images
    whole = lambda array: pl.BlockSpec(array.shape, lambda i, *_: (0,) * array.ndim)
    image = lambda *dims: pl.BlockSpec((1,) + dims, lambda i, *_: (i,) + (0,) * len(dims))
    return pl.pallas_call(
        attention_backward_kernel,
        grid_spec=pltpu.PrefetchScalarGridSpec(
            num_scalar_prefetch=2,
            grid=(images,),
            in_specs=[
                pl.BlockSpec((1, length, width), lambda i, *_: (first + i, 0, 0)),
                pl.BlockSpec((1, length, width), lambda i, *_: (first + i, 0, 0)),
                whole(side_a),
                whole(side_b),
                whole(gains),
                pl.BlockSpec((1, length, 2), lambda i, *_: (first + i, 0, 0)),
                image(length, 3 * width),
                image(heads, length, length),
                image(length, width),
                image(length, 4 * NARROW),
                image(length, width),
                whole(home),
            ],
            out_specs=[
                image(length, width),
                pl.BlockSpec((width, 4 * NARROW), lambda i, *_: (0, 0)),
                pl.BlockSpec((width, 4 * NARROW), lambda i, *_: (0, 0)),
            ],
            scratch_shapes=[pltpu.VMEM((length, 3 * width), BF16), pltpu.VMEM((length, width), BF16)],
        ),
        out_shape=[
            jax.ShapeDtypeStruct((images, length, width), BF16),
            jax.ShapeDtypeStruct((width, 4 * NARROW), F32),
            jax.ShapeDtypeStruct((width, 4 * NARROW), F32),
        ],
        compiler_params=pltpu.CompilerParams(vmem_limit_bytes=VMEM_LIMIT),
        name="attention_backward",
    )(adapt, count, x4, cot4, side_a, side_b, gains, slots_col, qkv, weights, mixed, narrow, hidden, home)


def dispatch_kernel(count_ref, cot_ref, slots_ref, meta_ref, out_ref):
    micro = pl.program_id(0)
    images, length, width = cot_ref.shape
    experts, padded, _ = out_ref.shape
    slot_ids = lax.broadcasted_iota(jnp.int32, (experts * padded, length), 0)
    rows = None
    meta = None
    for image in range(images):
        hits = [(slot_ids == slots_ref[image, k : k + 1, :]).astype(F32).astype(BF16) for k in range(2)]
        live = jnp.where(image < count_ref[micro], 1.0, 0.0).astype(F32)
        delta = (cot_ref[image].astype(F32) * live).astype(BF16)
        term = mm(hits[0] + hits[1], delta)
        extra = mm(hits[0], meta_ref[image, 0]) + mm(hits[1], meta_ref[image, 1])
        rows = term if rows is None else rows + term
        meta = extra if meta is None else meta + extra
    out_ref[:, :, :width] = rows.astype(BF16).reshape(experts, padded, width)
    out_ref[:, :, width:] = meta.astype(BF16).reshape(experts, padded, LANES)


def dispatch(counts, cot4, slots_row, meta, experts, padded):
    micros = counts.shape[0]
    total, length, width = cot4.shape
    images = total // micros
    return pl.pallas_call(
        dispatch_kernel,
        grid_spec=pltpu.PrefetchScalarGridSpec(
            num_scalar_prefetch=1,
            grid=(micros,),
            in_specs=[
                pl.BlockSpec((images, length, width), lambda i, *_: (i, 0, 0)),
                pl.BlockSpec((images, 2, length), lambda i, *_: (i, 0, 0)),
                pl.BlockSpec((images, 2, length, LANES), lambda i, *_: (i, 0, 0, 0)),
            ],
            out_specs=pl.BlockSpec((experts, padded, width + LANES), lambda i, *_: (0, i, 0)),
        ),
        out_shape=jax.ShapeDtypeStruct((experts, micros * padded, width + LANES), BF16),
        compiler_params=pltpu.CompilerParams(vmem_limit_bytes=VMEM_LIMIT),
        name="dispatch",
    )(counts, cot4, slots_row, meta)


def output_kernel(count_ref, hidden_ref, slots_ref, home_ref, out_ref):
    step = pl.program_id(0)
    length = hidden_ref.shape[1]
    slots = home_ref.shape[0] * home_ref.shape[1]
    slot_ids = lax.broadcasted_iota(jnp.int32, (length, slots), 1)
    hit = jnp.logical_or(slot_ids == slots_ref[0, :, 0:1], slot_ids == slots_ref[0, :, 1:2])
    mixture = mm(hit.astype(F32).astype(BF16), home_ref[...].reshape(slots, home_ref.shape[2]))
    live = jnp.where(step < count_ref[0], 1.0, 0.0).astype(F32)
    out_ref[0] = ((hidden_ref[0] + mixture) * live).astype(BF16)


def combine_output(micro, count, hidden, slots_col, home):
    images, length, width = hidden.shape
    first = micro * images
    return pl.pallas_call(
        output_kernel,
        grid_spec=pltpu.PrefetchScalarGridSpec(
            num_scalar_prefetch=1,
            grid=(images,),
            in_specs=[
                pl.BlockSpec((1, length, width), lambda i, *_: (i, 0, 0)),
                pl.BlockSpec((1, length, 2), lambda i, *_: (first + i, 0, 0)),
                pl.BlockSpec(home.shape, lambda i, *_: (0, 0, 0)),
            ],
            out_specs=pl.BlockSpec((1, length, width), lambda i, *_: (i, 0, 0)),
        ),
        out_shape=jax.ShapeDtypeStruct((images, length, width), BF16),
        compiler_params=pltpu.CompilerParams(vmem_limit_bytes=VMEM_LIMIT),
        name="combine_output",
    )(count, hidden, slots_col, home)


ERF_P = 0.3275911
ERF_A = (0.254829592, -0.284496736, 1.421413741, -1.453152027, 1.061405429)


def gelu_pair(value):
    bell = jnp.exp(value * value * -0.5)
    ratio = 1.0 / (1.0 + jnp.abs(value) * (ERF_P / math.sqrt(2.0)))
    poly = ERF_A[4]
    for coefficient in ERF_A[3::-1]:
        poly = poly * ratio + coefficient
    tail = poly * ratio * bell * 0.5
    share = jnp.where(value < 0.0, tail, 1.0 - tail)
    return value * share, share + value * bell * (1.0 / math.sqrt(2.0 * math.pi))


def expert_kernel(
    place_ref, rows_ref, arrived_ref, router_ref, *refs, parts, first_call,
):
    count = 2 * parts - 1
    ins, outs, smalls = refs[:count], refs[count : 2 * count], refs[2 * count : 3 * count]
    refs = refs[3 * count :]
    if not first_call:
        old_wide_ref, old_tall_ref = refs[:2]
        refs = refs[2:]
    (result_ref, sent_ref, wide_ref, tall_ref,
     in_s, out_s, tall_s, flat_s, sem) = refs
    step = pl.program_id(0)
    half, padded, width = rows_ref.shape
    hidden_units = in_s.shape[1]
    piece = hidden_units // parts
    shard = width // parts
    total = half * padded

    def source(holder, part):
        return 0 if part == holder else (part - holder if part > holder else parts - 1 + holder - part)

    @pl.when(step == 0)
    def _():
        for holder in range(parts):
            @pl.when(place_ref[0] == holder)
            def _(holder=holder):
                copies = []
                for part in range(parts):
                    which = source(holder, part)
                    copies += [
                        pltpu.make_async_copy(ins[which], in_s.at[pl.ds(part * shard, shard)], sem),
                        pltpu.make_async_copy(outs[which], out_s.at[pl.ds(part * piece, piece)], sem),
                        pltpu.make_async_copy(
                            smalls[which].at[pl.ds(0, piece)], tall_s.at[pl.ds(part * piece, piece)], sem
                        ),
                        pltpu.make_async_copy(
                            smalls[which].at[pl.ds(piece, shard)], flat_s.at[pl.ds(part * shard, shard)], sem
                        ),
                    ]
                for copy in copies:
                    copy.start()
                for copy in copies:
                    copy.wait()

        if first_call:
            wide_ref[...] = jnp.zeros_like(wide_ref)
            tall_ref[...] = jnp.zeros_like(tall_ref)
        else:
            wide_ref[...] = old_wide_ref[...]
            tall_ref[...] = old_tall_ref[...]

    rows = rows_ref[...].reshape(total, width)
    delta = arrived_ref[:, :, :width].reshape(total, width)
    meta = arrived_ref[:, :, width:].reshape(total, LANES).astype(F32)
    lane = lax.broadcasted_iota(jnp.int32, (total, LANES), 1).astype(F32)
    lane_owner = lane_adapter((total, NARROW)).astype(F32)
    select = jnp.where(jnp.logical_and(lane_owner == meta[:, 0:1], meta[:, 2:3] > 0.5), 1.0, 0.0)
    own_expert = place_ref[1].astype(F32)
    is_own = (lane == own_expert).astype(F32)
    is_other = (lane == meta[:, 1:2]).astype(F32)
    logits = mm(rows, router_ref[...])
    own_logit = jnp.sum(logits * is_own, axis=-1, keepdims=True)
    other_logit = jnp.sum(logits * is_other, axis=-1, keepdims=True)
    peak = jnp.maximum(own_logit, other_logit)
    own_exp, other_exp = jnp.exp(own_logit - peak), jnp.exp(other_logit - peak)
    norm = 1.0 / (own_exp + other_exp)
    gate, other_gate = own_exp * norm, other_exp * norm
    grad_result = (delta.astype(F32) * gate).astype(BF16)

    thin_in = (mm(rows, flat_s[:, :NARROW]) * select).astype(BF16)
    grad_thin_out = (mm(grad_result, flat_s[:, NARROW:]) * select).astype(BF16)
    result = thin_out = sent = grad_thin_in = None
    for part in range(parts):
        cols = slice(part * piece, (part + 1) * piece)
        in_part = in_s[:, cols]
        out_part = out_s[cols, :]
        up_in_t = tall_s[cols, :NARROW]
        down_out = tall_s[cols, NARROW:]
        lifted = mm(rows, in_part) + mm_nt(thin_in, up_in_t)
        value, slope = gelu_pair(lifted)
        active = value.astype(BF16)
        grad_active = mm_nt(grad_result, out_part) + mm_nt(grad_thin_out, down_out)
        grad_lifted = (grad_active * slope).astype(BF16)
        terms = (mm(active, out_part), mm(active, down_out), mm_nt(grad_lifted, in_part), mm(grad_lifted, up_in_t))
        if part == 0:
            result, thin_out, sent, grad_thin_in = terms
        else:
            result, thin_out, sent, grad_thin_in = (
                result + terms[0], thin_out + terms[1], sent + terms[2], grad_thin_in + terms[3]
            )
        wide_ref[part, 0] = wide_ref[part, 0] + mm_tn(thin_in, grad_lifted)
        wide_ref[part, 1] = wide_ref[part, 1] + mm_tn(grad_thin_out, active)
    thin_out = (thin_out * select).astype(BF16)
    grad_thin_in = (grad_thin_in * select).astype(BF16)
    result = (result + mm_nt(thin_out, flat_s[:, NARROW:])).astype(BF16).astype(F32)
    sent = sent + mm_nt(grad_thin_in, flat_s[:, :NARROW])
    tall_ref[:, :NARROW] = tall_ref[:, :NARROW] + mm_tn(rows, grad_thin_in)
    tall_ref[:, NARROW:] = tall_ref[:, NARROW:] + mm_tn(grad_result, thin_out)
    result_ref[...] = (result * gate).astype(BF16).reshape(half, padded, width)
    grad_gate = jnp.sum(delta.astype(F32) * result, axis=-1, keepdims=True)
    pull = (is_own - is_other) * (gate * other_gate * grad_gate)
    high = pull.astype(BF16)
    rest = (pull - high.astype(F32)).astype(BF16)
    sent = sent + (mm_nt(high, router_ref[...]) + mm_nt(rest, router_ref[...]))
    sent_ref[...] = sent.astype(BF16).reshape(half, padded, width)


def expert_step(micro, place, rows, arrived, router, pieces, old):
    experts, padded, width = rows.shape
    ins, outs, smalls = pieces
    parts = (len(ins) + 1) // 2
    hidden_units = ins[0].shape[1]
    piece = hidden_units // parts
    blocks = 2
    half = experts // blocks
    hbm = pl.BlockSpec(memory_space=pl.ANY)
    wide = jax.ShapeDtypeStruct((parts, 2, NARROW, piece), F32)
    tall = jax.ShapeDtypeStruct((width, 2 * NARROW), F32)
    whole = lambda array: pl.BlockSpec(array.shape, lambda i, *_: (0,) * len(array.shape))
    block = pl.BlockSpec((half, padded, width), lambda i, *_: (i, 0, 0))
    extra = [] if old is None else list(old)
    return pl.pallas_call(
        functools.partial(expert_kernel, parts=parts, first_call=old is None),
        grid_spec=pltpu.PrefetchScalarGridSpec(
            num_scalar_prefetch=1,
            grid=(blocks,),
            in_specs=[
                block,
                pl.BlockSpec((half, padded, width + LANES), lambda i, *_: (i, micro, 0)),
                whole(router),
            ]
            + [hbm] * (len(ins) + len(outs) + len(smalls))
            + [whole(array) for array in extra],
            out_specs=[block, block, whole(wide), whole(tall)],
            scratch_shapes=[
                pltpu.VMEM((width, hidden_units), BF16),
                pltpu.VMEM((hidden_units, width), BF16),
                pltpu.VMEM((hidden_units, 2 * NARROW), BF16),
                pltpu.VMEM((width, 2 * NARROW), BF16),
                pltpu.SemaphoreType.DMA,
            ],
        ),
        out_shape=[
            jax.ShapeDtypeStruct((experts, padded, width), BF16),
            jax.ShapeDtypeStruct((experts, padded, width), BF16),
            wide,
            tall,
        ],
        compiler_params=pltpu.CompilerParams(vmem_limit_bytes=VMEM_LIMIT),
        name="expert_step",
    )(place, rows, arrived, router, *ins, *outs, *smalls, *extra)


def line_gather(array, size):
    down, up = [], []
    moving = array
    for step in range(1, size):
        moving = lax.ppermute(moving, "dp", [(i, i - 1) for i in range(1, size - step + 1)])
        down.append(moving)
    moving = array
    for step in range(1, size):
        moving = lax.ppermute(moving, "dp", [(i, i + 1) for i in range(step - 1, size - 1)])
        up.append(moving)
    return [array] + down + up


def line_stack(pieces, size):
    place = lax.axis_index("dp")
    ordered = []
    for part in range(size):
        chosen = None
        for holder in range(size):
            which = 0 if part == holder else (part - holder if part > holder else size - 1 + holder - part)
            chosen = pieces[which] if chosen is None else jnp.where(place == holder, pieces[which], chosen)
        ordered.append(chosen)
    return jnp.stack(ordered)


def line_scatter(own, size):
    place = lax.axis_index("dp")
    pick = lambda index: lax.dynamic_index_in_dim(own, jnp.clip(index, 0, size - 1), 0, keepdims=False)
    total = pick(place).astype(F32)
    for sign in (1, -1):
        arriving = None
        for step in range(1, size):
            message = pick(place + sign * (size - step))
            if arriving is not None:
                message = (message.astype(F32) + arriving.astype(F32)).astype(BF16)
            edges = [(i, i + 1) if sign > 0 else (size - 1 - i, size - 2 - i) for i in range(step)]
            arriving = lax.ppermute(message, "dp", edges)
        total = total + arriving.astype(F32)
    return total


def swap(array, bit, size):
    return lax.ppermute(array, "expert", [(i, i ^ bit) for i in range(size)])


def dense_gather(packed, half, size_dp, size_expert):
    rows = packed.shape[0]
    if size_expert < 4 or size_expert & (size_expert - 1) or (2 * rows) % 8:
        full = lax.all_gather(packed, ("dp", "expert"), axis=0, tiled=True)
        return full[:, :half], full[:, half:]
    place = lax.axis_index("expert")
    core = place % 2
    low, high = packed[:, :half], packed[:, half:]
    kept = jnp.where(core == 0, low, high)
    other = swap(jnp.where(core == 0, high, low), 1, size_expert)
    pair = jnp.concatenate([jnp.where(core == 0, kept, other), jnp.where(core == 0, other, kept)], axis=0)
    pieces = line_gather(pair, size_dp)
    stacked = line_stack(pieces, size_dp)
    bits = [1 << b for b in range(1, size_expert.bit_length() - 1)]
    cut = (half // LANES + 1) // 2 * LANES
    done = []
    for stream, order in ((stacked[:, :, :cut], bits), (stacked[:, :, cut:], bits[::-1])):
        held = []
        for bit in order:
            axis = 1 + sum(1 for other_bit in held if other_bit > bit)
            arrived = swap(stream, bit, size_expert)
            mine = (place // bit) % 2 == 0
            stream = jnp.stack([jnp.where(mine, stream, arrived), jnp.where(mine, arrived, stream)], axis=axis)
            held.append(bit)
        done.append(stream.reshape(-1, stream.shape[-1]))
    side = jnp.concatenate(done, axis=1)
    arrived = swap(side, 1, size_expert)
    return jnp.where(core == 0, side, arrived), jnp.where(core == 0, arrived, side)


def full_scatter(own, size_dp, size_expert):
    rows = own.shape[0] // (size_dp * size_expert)
    if size_expert < 4 or size_expert & (size_expert - 1) or rows % 8:
        return lax.psum_scatter(own.astype(F32), ("dp", "expert"), scatter_dimension=0, tiled=True)
    place = lax.axis_index("expert")
    columns = own.shape[1]
    bits = [1 << b for b in range(1, size_expert.bit_length() - 1)]

    def halve(array, axis, bit):
        side = (place // bit) % 2
        mine = lax.dynamic_index_in_dim(array, side, axis, keepdims=False)
        other = lax.dynamic_index_in_dim(array, 1 - side, axis, keepdims=False)
        return (mine.astype(F32) + swap(other, bit, size_expert).astype(F32)).astype(BF16)

    grid = own.reshape((size_dp,) + (2,) * (len(bits) + 1) + (rows, columns))
    grid = halve(grid, len(bits) + 1, 1)
    cut = (columns // LANES + 1) // 2 * LANES
    done = []
    for stream, order in ((grid[..., :cut], bits), (grid[..., cut:], bits[::-1])):
        left = list(bits[::-1])
        for bit in order:
            stream = halve(stream, 1 + left.index(bit), bit)
            left.remove(bit)
        done.append(stream)
    return line_scatter(jnp.concatenate(done, axis=-1), size_dp)


def exchange(array):
    return lax.all_to_all(array, "expert", split_axis=0, concat_axis=0, tiled=True)


def shards(
    tokens, image_count, adapter_index, expert_ids, norm_gains, attention_in, attention_out, router,
    expert_in, expert_out, attention_down, attention_up, expert_down_in, expert_up_in,
    expert_down_out, expert_up_out, cotangent,
):
    micros, images, length, width = tokens.shape
    size_dp = lax.axis_size("dp")
    experts = lax.axis_size("expert")
    hidden_units = expert_in.shape[2]
    rows = images * length
    capacity = capacity_of(rows, experts)
    padded = -(-capacity // 16) * 16
    shard_rows = attention_in.shape[0]

    half = 2 * width + 4 * NARROW + LANES
    small = jnp.concatenate([router, norm_gains.T], axis=1)
    small = jnp.pad(small, ((0, 0), (0, LANES - small.shape[1])))
    packed = jnp.concatenate(
        [
            attention_in[:, : 2 * width],
            attention_down.reshape(shard_rows, 4 * NARROW),
            small,
            attention_in[:, 2 * width :],
            attention_out,
            attention_up.reshape(4 * NARROW, shard_rows).T,
            jnp.zeros((shard_rows, LANES), BF16),
        ],
        axis=1,
    )
    side_a, side_b = dense_gather(packed, half, size_dp, experts)
    tail = side_a[:, 2 * width + 4 * NARROW :]
    gains = tail[:, experts : experts + 2].astype(F32).T
    router_full = jnp.where(jnp.arange(LANES)[None, :] < experts, tail, jnp.zeros_like(tail))

    own_in = expert_in[0]
    own_out = expert_out[0]
    own_small = jnp.concatenate(
        [
            jnp.concatenate(
                [
                    expert_up_in[0].reshape(NARROW, -1).T,
                    expert_down_out[0].reshape(-1, NARROW),
                ],
                axis=1,
            ),
            jnp.concatenate(
                [
                    expert_down_in[0].reshape(-1, NARROW),
                    expert_up_out[0].reshape(NARROW, -1).T,
                ],
                axis=1,
            ),
        ],
        axis=0,
    )
    pieces = (line_gather(own_in, size_dp), line_gather(own_out, size_dp), line_gather(own_small, size_dp))

    picks = expert_ids.reshape(micros, 2 * rows)
    hits = (picks[:, :, None] == jnp.arange(experts, dtype=jnp.int32)).astype(jnp.int32)
    placed = jnp.sum((jnp.cumsum(hits, axis=1) - 1) * hits, axis=2)
    slots_col = (picks * padded + placed).reshape(micros * images, length, 2)
    slots_row = jnp.swapaxes(slots_col, 1, 2)
    ids4 = expert_ids.reshape(micros * images, length, 2)
    lane = jnp.arange(LANES, dtype=jnp.int32)
    adapt4 = adapter_index.reshape(micros * images)
    other = jnp.swapaxes(ids4[:, :, ::-1], 1, 2)[..., None]
    meta = jnp.where(
        lane == 0,
        adapt4[:, None, None, None],
        jnp.where(lane == 1, other, jnp.where(lane == 2, 1, 0)),
    ).astype(BF16)
    x4 = tokens.reshape(micros * images, length, width)
    cot4 = cotangent.reshape(micros * images, length, width)
    counts = image_count.reshape(micros)
    arrived = exchange(dispatch(counts, cot4, slots_row, meta, experts, padded))

    place = jnp.stack([lax.axis_index("dp"), lax.axis_index("expert")]).astype(jnp.int32)
    kept, received = [], []
    for micro in range(micros):
        *saved, sent = attention_forward(
            micro, adapter_index[micro], x4, side_a, side_b, gains, slots_row, experts, padded
        )
        kept.append(saved)
        received.append(exchange(sent))
    old = None
    results, backs = [], []
    for micro in range(micros):
        result, back, *old = expert_step(micro, place, received[micro], arrived, router_full, pieces, old)
        backs.append(exchange(back))
        results.append(result)
    outputs, input_grads, down_total, up_total = [], [], None, None
    for micro in range(micros):
        input_grad, down_new, up_new = attention_backward(
            micro, adapter_index[micro], image_count[micro], x4, cot4, side_a, side_b, gains,
            slots_col, kept[micro], backs[micro],
        )
        input_grads.append(input_grad)
        down_total = down_new if down_total is None else down_total + down_new
        up_total = up_new if up_total is None else up_total + up_new
    for micro in range(micros):
        outputs.append(
            combine_output(micro, image_count[micro], kept[micro][4], slots_col, exchange(results[micro]))
        )

    wide, tall = old
    piece, shard = hidden_units // size_dp, width // size_dp
    wide = line_scatter(wide.astype(BF16), size_dp)
    tall = line_scatter(tall.astype(BF16).reshape(size_dp, shard, 2 * NARROW), size_dp)
    dense = full_scatter(
        jnp.concatenate([down_total, up_total], axis=1).astype(BF16), size_dp, experts
    )
    return (
        jnp.stack(outputs),
        jnp.stack(input_grads),
        dense[:, : 4 * NARROW].reshape(shard_rows, 4, ADAPTERS, RANK),
        dense[:, 4 * NARROW :].T.reshape(4, ADAPTERS, RANK, shard_rows),
        tall[:, :NARROW].reshape(1, shard, ADAPTERS, RANK),
        wide[0].reshape(1, ADAPTERS, RANK, piece),
        wide[1].T.reshape(1, piece, ADAPTERS, RANK),
        tall[:, NARROW:].T.reshape(1, ADAPTERS, RANK, shard),
    )


def solution(mesh):
    everywhere = ("dp", "expert")
    return jax.shard_map(
        shards,
        mesh=mesh,
        in_specs=(
            P(None, everywhere, None, None),
            P(None, everywhere),
            P(None, everywhere),
            P(None, everywhere, None, None),
            P(None, everywhere),
            P(everywhere, None),
            P(everywhere, None),
            P(everywhere, None),
            P("expert", "dp", None),
            P("expert", "dp", None),
            P(everywhere, None, None, None),
            P(None, None, None, everywhere),
            P("expert", "dp", None, None),
            P("expert", None, None, "dp"),
            P("expert", "dp", None, None),
            P("expert", None, None, "dp"),
            P(None, everywhere, None, None),
        ),
        out_specs=(
            P(None, everywhere, None, None),
            P(None, everywhere, None, None),
            P(everywhere, None, None, None),
            P(None, None, None, everywhere),
            P("expert", "dp", None, None),
            P("expert", None, None, "dp"),
            P("expert", "dp", None, None),
            P("expert", None, None, "dp"),
        ),
        check_vma=False,
    )
```

time: 1770 us -> 635 us (0.36)
  blocking collectives: 740 us -> 0 us
  local copies, waits for them, and re-layouts: 347 us -> 43.4 us
  matrix products: 268 us -> 0 us
  Pallas kernels: 0 us -> 185 us
  starting transfers between devices: 44 us -> 134 us
  waiting for transfers between devices: 259 us -> 220 us
  other arithmetic: 77.1 us -> 40.4 us
    all_gather x16 -> x0, blocking collectives: 740 us -> none  [the longest x2 195 us: dense_fetch(): lax.all_gather(attention_up, ('dp', 'expert'), axis=3, tiled=True)]
    dot_general x92 -> x0, matrix products: 268 us -> none  [the longest x30 119 us: matmul(): return jnp.dot(left, right, preferred_element_type=jnp.float32)]
    ppermute x0 -> x53, waiting for transfers between devices: none -> 210 us  [the longest x12 171 us: line_gather(): lax.ppermute(moving, 'dp', [(i, i - 1) for i in range(1, size - step + 1)])]
    unnamed x10 -> x0, waiting for transfers between devices: 206 us -> none
    pallas_call x0 -> x9, Pallas kernels: none -> 185 us  [the longest x2 83.5 us: expert_step(): pl.pallas_call(functools.partial(expert_kernel, parts=parts, first_call=o...]
    ppermute x0 -> x53, starting transfers between devices: none -> 105 us  [the longest x18 47 us: line_scatter(): arriving = lax.ppermute(message, 'dp', edges)]
    reshape x42 -> x4, local copies, waits for them, and re-layouts: 72.4 us -> 5.28 us  [the longest x2 3.32 us: dense_gather(): done.append(stream.reshape(-1, stream.shape[-1]))]
    while x450 -> x0, local copies, waits for them, and re-layouts: 54 us -> none
  transfers between devices with their start and end apart: 24 -> 60, of which waited for: 7 -> 18; matrix products, arithmetic and copies ran while one was open for 29% -> 10% of each run, Pallas kernels for 0% -> 30%
where the time goes in v1:
time: 635 us; the launch traced here: 625 us
  waiting for transfers between devices  220 us (35%)
  Pallas kernels  185 us (29%)
  starting transfers between devices  134 us (21%)
  local copies, waits for them, and re-layouts  43.4 us (7%)
  other arithmetic  40.4 us (6%)
    ppermute x12, waiting for transfers between devices, line_gather(): lax.ppermute(moving, 'dp', [(i, i - 1) for i in range(1, size - step + 1)])  171 us
    pallas_call x2, Pallas kernels, expert_step(): pl.pallas_call(functools.partial(expert_kernel, parts=parts, first_call=o...  83.5 us
    pallas_call x2, Pallas kernels, attention_backward(): pl.pallas_call(attention_backward_kernel, grid_spec=pltpu.PrefetchScalarG...  54.8 us
    ppermute x18, starting transfers between devices, line_scatter(): arriving = lax.ppermute(message, 'dp', edges)  47 us
    pallas_call x2, Pallas kernels, attention_forward(): pl.pallas_call(attention_forward_kernel, grid_spec=pltpu.PrefetchScalarGr...  32.8 us
    ppermute x12, starting transfers between devices, line_gather(): lax.ppermute(moving, 'dp', [(i, i + 1) for i in range(step - 1, size - 1)])  30.4 us
    ppermute x11, waiting for transfers between devices, swap(): return lax.ppermute(array, 'expert', [(i, i ^ bit) for i in range(size)])  29.8 us
    all_to_all x7, starting transfers between devices, exchange(): lax.all_to_all(array, 'expert', split_axis=0, concat_axis=0, tiled=True)  28.6 us
  transfers between devices with their start and end apart: 60, of which 18 were waited for; matrix products, arithmetic and copies ran while one was open for 10% of the time, Pallas kernels for 30%

profile of v1, /device:TPU:0, one launch (start us, length us, event | category | flops | bytes accessed | tf_op | source)
XLA Modules:
  0.0 625.3 jit_solution(3667356664760949525)
XLA Ops:
  9.1 4.8 collective-permute-start.1
  24.7 6.1 collective-permute-done.5
  32.1 6.4 %collective-permute-done.6 = bf16[48,2176]{1,0:T(8,128)(2,1)S(1)} collective-permute-done((bf16[48,2176]{1,0:T(8,128)(2,1)S(1)}, bf16[48,2176]{1,0:T(8,128)(2,1)S(1)}, u32[]{:S(2)}, u32[]{:S(2)}) %collective-permute-start.6) | collective-permute-done | bytes 208928 | tf_op jit(solution)/shard_map/ppermute | solution.py:550
  42.2 4.9 collective-permute-done.9
  48.9 4.0 collective-permute-done.7
  54.8 11.6 %collective-permute-done.10 = bf16[4,2,48,1024]{3,2,0,1:T(8,128)(2,1)S(1)} collective-permute-done((bf16[4,2,48,1024]{3,2,0,1:T(8,128)(2,1)S(1)}, bf16[4,2,48,1024]{3,2,0,1:T(8,128)(2,1)S(1)}, u32[]{:S(2)}, u32[]{:S(2)}) %collective-permute-start.10) | collective-permute-done | bytes 786464 | tf_op jit(solution)/shard_map/ppermute | solution.py:588
  86.9 6.0 dispatch.1
  97.8 5.6 collective-permute-start.15
  104.9 5.6 collective-permute-start.21
  120.5 4.8 broadcast_select_fusion
  125.3 37.6 %collective-permute-done.24.refs_15_ = bf16[960,256]{1,0:T(8,128)(2,1)} collective-permute-done((bf16[960,256]{1,0:T(8,128)(2,1)}, bf16[960,256]{1,0:T(8,128)(2,1)}, u32[]{:S(2)}, u32[]{:S(2)}) %collective-permute-start.24) | collective-permute-done | bytes 491552 | tf_op jit(solution)/shard_map/ppermute | solution.py:550
  166.8 5.5 copy.114.a_ref
  172.3 5.5 copy.115.b_ref
  177.8 16.4 %attention_forward.2 = (bf16[2,197,2304]{2,1,0:T(8,128)(2,1)}, bf16[2,12,197,197]{3,2,1,0:T(8,128)(2,1)}, bf16[2,197,768]{2,1,0:T(8,128)(2,1)}, bf16[2,197,512]{...) custom-call(s32[2]{0:T(128)} %get-tuple-element.124.adapt_ref, bf16[4,197,768]{2,1,0:T(8,128)(2,1)} %bitcast.186, ...), custom_call_target="tpu_custom_call" | custom-call | tf_op jit(solution)/shard_map/attention_forward/pallas_call | solution.py:128
  194.2 4.3 all-to-all-start
  205.9 58.9 %collective-permute-done.25.refs_16_ = bf16[960,256]{1,0:T(8,128)(2,1)} collective-permute-done((bf16[960,256]{1,0:T(8,128)(2,1)}, bf16[960,256]{1,0:T(8,128)(2,1)}, u32[]{:S(2)}, u32[]{:S(2)}) %collective-permute-start.25) | collective-permute-done | bytes 491552 | tf_op jit(solution)/shard_map/ppermute | solution.py:550
  266.2 16.4 %attention_forward.3 = (bf16[2,197,2304]{2,1,0:T(8,128)(2,1)}, bf16[2,12,197,197]{3,2,1,0:T(8,128)(2,1)}, bf16[2,197,768]{2,1,0:T(8,128)(2,1)}, bf16[2,197,512]{...) custom-call(s32[2]{0:T(128)} %get-tuple-element.125.adapt_ref, bf16[4,197,768]{2,1,0:T(8,128)(2,1)} %bitcast.187, ...), custom_call_target="tpu_custom_call" | custom-call | tf_op jit(solution)/shard_map/attention_forward/pallas_call | solution.py:128
  293.8 59.0 %collective-permute-done.26.refs_17_ = bf16[960,256]{1,0:T(8,128)(2,1)S(1)} collective-permute-done((bf16[960,256]{1,0:T(8,128)(2,1)}, bf16[960,256]{1,0:T(8,128)(2,1)S(1)}, u32[]{:S(2)}, u32[]{:S(2)}) %collective-permute-start.26) | collective-permute-done | bytes 491552 | tf_op jit(solution)/shard_map/ppermute | solution.py:550
  357.7 41.0 %expert_step.2 = (bf16[8,112,768]{2,1,0:T(8,128)(2,1)}, bf16[8,112,768]{2,1,0:T(8,128)(2,1)}, f32[4,2,128,768]{3,2,1,0:T(8,128)}, f32[768,256]{1,0:T(8,128)}) custom-call(s32[2]{0:T(128)} %pad_add_fusion.place_ref, bf16[8,112,768]{2,1,0:T(8,128)(2,1)} %all-to-all-done.rows_ref, bf16[8,224,896]{2,1,0:T(8,128)(2,1)} %copy-done, ...), custom_call_target="tpu_custom_call" | custom-call | tf_op jit(solution)/shard_map/expert_step/pallas_call | solution.py:514
  402.5 42.5 %expert_step.3 = (bf16[8,112,768]{2,1,0:T(8,128)(2,1)}, bf16[8,112,768]{2,1,0:T(8,128)(2,1)}, f32[4,2,128,768]{3,2,1,0:T(8,128)}, f32[768,256]{1,0:T(8,128)}) custom-call(s32[2]{0:T(128)} %pad_add_fusion.place_ref, bf16[8,112,768]{2,1,0:T(8,128)(2,1)} %copy-done.6, bf16[8,224,896]{2,1,0:T(8,128)(2,1)} %copy-done, bf16[768,128]{1,0:T(8,128)(2,1)} %copy.124.router_ref, ...), custom_call_target="tpu_custom_call" | custom-call | tf_op jit(solution)/shard_map/expert_step/pallas_call | solution.py:514
  445.1 4.4 all-to-all-start.6
  454.1 4.2 collective-permute-start.42
  458.2 10.2 %all-to-all-done.6.home_ref = bf16[8,112,768]{2,1,0:T(8,128)(2,1)} async-done(((bf16[8,112,768]{2,1,0:T(8,128)(2,1)}), bf16[8,112,768]{2,1,0:T(8,128)(2,1)}, u32[]{:S(2)}, u32[]{:S(2)}) %all-to-all-start.6) | async-done | bytes 1376288 | tf_op jit(solution)/shard_map/all_to_all | solution.py:649
  468.5 4.3 all-to-all-start.2
  485.5 5.1 collective-permute-start.48
  490.6 27.2 %attention_backward.2 = (bf16[2,197,768]{2,1,0:T(8,128)(2,1)}, f32[768,512]{1,0:T(8,128)}, f32[768,512]{1,0:T(8,128)}) custom-call(s32[2]{0:T(128)} %get-tuple-element.124.adapt_ref, s32[1]{0:T(128)} %bitcast.count_ref, bf16[4,197,768]{2,1,0:T(8,128)(2,1)} %bitcast.188, bf16[4,197,768]{2,1,0:T(8,128)(2,1)} %bitcast.191, bf16[768,2176]{1,0:T(8,128)(2,1)} %copy.114.a_ref, ...), custom_call_target="tpu_custom_call" | custom-call | tf_op jit(solution)/shard_map/attention_backward/pallas_call | solution.py:269
  517.8 27.6 %attention_backward.3 = (bf16[2,197,768]{2,1,0:T(8,128)(2,1)}, f32[768,512]{1,0:T(8,128)}, f32[768,512]{1,0:T(8,128)}) custom-call(s32[2]{0:T(128)} %get-tuple-element.125.adapt_ref, s32[1]{0:T(128)} %bitcast.44.count_ref, bf16[4,197,768]{2,1,0:T(8,128)(2,1)} %bitcast.189, bf16[4,197,768]{2,1,0:T(8,128)(2,1)} %bitcast.192, bf16[768,2176]{1,0:T(8,128)(2,1)} %copy.114.a_ref, ...), custom_call_target="tpu_custom_call" | custom-call | tf_op jit(solution)/shard_map/attention_backward/pallas_call | solution.py:269
  547.5 4.3 all-to-all-start.4
  567.6 4.1 combine_output.2
  571.6 4.1 combine_output.3
  590.9 9.8 %collective-permute-start.35 = (bf16[24,1024]{1,0:T(8,128)(2,1)S(1)}, bf16[24,1024]{1,0:T(8,128)(2,1)S(1)}, u32[]{:S(2)}, u32[]{:S(2)}) collective-permute-start(bf16[24,1024]{1,0:T(8,128)(2,1)S(1)} %get-tuple-element.120), channel_id=1, source_target_pairs={{0,8},{1,9},{2,10},{3,11},{4,12},{5,13},{6,14},{7,15}} | collective-permute-start | bytes 147464 | tf_op jit(solution)/shard_map/ppermute | solution.py:582
  609.0 8.4 %collective-permute-start.37 = (bf16[24,1024]{1,0:T(8,128)(2,1)S(1)}, bf16[24,1024]{1,0:T(8,128)(2,1)S(1)}, u32[]{:S(2)}, u32[]{:S(2)}) collective-permute-start(bf16[24,1024]{1,0:T(8,128)(2,1)S(1)} %get-tuple-element.116), channel_id=1, source_target_pairs={{0,8},{8,16},{16,24},{1,9},{9,17},{17,25},{2,10},{10,18},{18,26},{... | collective-permute-start | bytes 147464 | tf_op jit(solution)/shard_map/ppermute | solution.py:582
  (246 shorter events, 162.6 us)
Async XLA Ops:
  77.3 41.9 %collective-permute-start.11 = (bf16[768,2176]{0,1:T(8,128)(2,1)}, bf16[768,2176]{0,1:T(8,128)(2,1)}, u32[]{:S(2)}, u32[]{:S(2)}) collective-permute-start(bf16[768,2176]{0,1:T(8,128)(2,1)} %pad_maximum_fusion), channel_id=1, source_target_pairs={{0,1},{1,0},{2,3},{3,2},{4,5},{5,4},{6,7},{7,6},{8,9},{9,8},{10,11... | collective-permute-start | bytes 10027016 | tf_op jit(solution)/shard_map/ppermute | solution.py:588
  92.9 101.3 %all-to-all-start.1 = ((bf16[8,224,896]{2,1,0:T(8,128)(2,1)}), bf16[8,224,896]{2,1,0:T(8,128)(2,1)S(1)}, u32[]{:S(2)}, u32[]{:S(2)}) async-start(bf16[8,224,896]{2,1,0:T(8,128)(2,1)} %dispatch.1), calls=%async_computation.1 | async-start | bytes 6422528 | tf_op jit(solution)/shard_map/all_to_all | solution.py:649
  96.5 102.0 %collective-permute-start.12 = (bf16[192,3072]{1,0:T(8,128)(2,1)}, bf16[192,3072]{1,0:T(8,128)(2,1)}, u32[]{:S(2)}, u32[]{:S(2)}) collective-permute-start(bf16[192,3072]{1,0:T(8,128)(2,1)} %bitcast.201), channel_id=1, source_target_pairs={{8,0},{16,8},{24,16},{9,1},{17,9},{25,17},{10,2},{18,10},{26,18},{... | collective-permute-start | bytes 3538952 | tf_op jit(solution)/shard_map/ppermute | solution.py:550
  97.8 102.0 %collective-permute-start.15 = (bf16[192,3072]{1,0:T(8,128)(2,1)}, bf16[192,3072]{1,0:T(8,128)(2,1)}, u32[]{:S(2)}, u32[]{:S(2)}) collective-permute-start(bf16[192,3072]{1,0:T(8,128)(2,1)} %bitcast.202), channel_id=1, source_target_pairs={{0,8},{8,16},{16,24},{1,9},{9,17},{17,25},{2,10},{10,18},{18,26},{... | collective-permute-start | bytes 3538952 | tf_op jit(solution)/shard_map/ppermute | solution.py:554
  103.4 98.1 %collective-permute-start.18 = (bf16[768,768]{1,0:T(8,128)(2,1)}, bf16[768,768]{1,0:T(8,128)(2,1)}, u32[]{:S(2)}, u32[]{:S(2)}) collective-permute-start(bf16[768,768]{1,0:T(8,128)(2,1)} %bitcast.205), channel_id=1, source_target_pairs={{8,0},{16,8},{24,16},{9,1},{17,9},{25,17},{10,2},{18,10},{26,18},{... | collective-permute-start | bytes 3538952 | tf_op jit(solution)/shard_map/ppermute | solution.py:550
  104.9 98.0 %collective-permute-start.21 = (bf16[768,768]{1,0:T(8,128)(2,1)}, bf16[768,768]{1,0:T(8,128)(2,1)}, u32[]{:S(2)}, u32[]{:S(2)}) collective-permute-start(bf16[768,768]{1,0:T(8,128)(2,1)} %bitcast.206), channel_id=1, source_target_pairs={{0,8},{8,16},{16,24},{1,9},{9,17},{17,25},{2,10},{10,18},{18,26},{... | collective-permute-start | bytes 3538952 | tf_op jit(solution)/shard_map/ppermute | solution.py:554
  119.2 43.7 %collective-permute-start.24 = (bf16[960,256]{1,0:T(8,128)(2,1)}, bf16[960,256]{1,0:T(8,128)(2,1)}, u32[]{:S(2)}, u32[]{:S(2)}) collective-permute-start(bf16[960,256]{1,0:T(8,128)(2,1)} %maximum_maximum_fusion.refs_14_), channel_id=1, source_target_pairs={{8,0},{16,8},{24,16},{9,1},{17,9},{25,17},{10,2},{18,10},{26,18},{... | collective-permute-start | bytes 1474568 | tf_op jit(solution)/shard_map/ppermute | solution.py:550
  162.9 41.7 %collective-permute-start.27 = (bf16[960,256]{1,0:T(8,128)(2,1)}, bf16[960,256]{1,0:T(8,128)(2,1)}, u32[]{:S(2)}, u32[]{:S(2)}) collective-permute-start(bf16[960,256]{1,0:T(8,128)(2,1)} %maximum_maximum_fusion.refs_14_), channel_id=1, source_target_pairs={{0,8},{8,16},{16,24},{1,9},{9,17},{17,25},{2,10},{10,18},{18,26},{... | collective-permute-start | bytes 1474568 | tf_op jit(solution)/shard_map/ppermute | solution.py:554
  194.2 88.4 %all-to-all-start = ((bf16[8,112,768]{2,1,0:T(8,128)(2,1)}), bf16[8,112,768]{2,1,0:T(8,128)(2,1)}, u32[]{:S(2)}, u32[]{:S(2)}) async-start(bf16[8,112,768]{2,1,0:T(8,128)(2,1)} %get-tuple-element.35), calls=%async_computation | async-start | bytes 2752512 | tf_op jit(solution)/shard_map/all_to_all | solution.py:649
  198.5 88.0 %collective-permute-start.13 = (bf16[192,3072]{1,0:T(8,128)(2,1)}, bf16[192,3072]{1,0:T(8,128)(2,1)}, u32[]{:S(2)}, u32[]{:S(2)}) collective-permute-start(bf16[192,3072]{1,0:T(8,128)(2,1)} %collective-permute-done.12.refs_1_), channel_id=1, source_target_pairs={{8,0},{16,8},{9,1},{17,9},{10,2},{18,10},{11,3},{19,11},{12,4},{20... | collective-permute-start | bytes 3538952 | tf_op jit(solution)/shard_map/ppermute | solution.py:550
  199.9 88.0 %collective-permute-start.16 = (bf16[192,3072]{1,0:T(8,128)(2,1)}, bf16[192,3072]{1,0:T(8,128)(2,1)}, u32[]{:S(2)}, u32[]{:S(2)}) collective-permute-start(bf16[192,3072]{1,0:T(8,128)(2,1)} %collective-permute-done.15.refs_4_), channel_id=1, source_target_pairs={{8,16},{16,24},{9,17},{17,25},{10,18},{18,26},{11,19},{19,27},{12,... | collective-permute-start | bytes 3538952 | tf_op jit(solution)/shard_map/ppermute | solution.py:554
  201.5 88.0 %collective-permute-start.19 = (bf16[768,768]{1,0:T(8,128)(2,1)}, bf16[768,768]{1,0:T(8,128)(2,1)}, u32[]{:S(2)}, u32[]{:S(2)}) collective-permute-start(bf16[768,768]{1,0:T(8,128)(2,1)} %collective-permute-done.18.refs_8_), channel_id=1, source_target_pairs={{8,0},{16,8},{9,1},{17,9},{10,2},{18,10},{11,3},{19,11},{12,4},{20... | collective-permute-start | bytes 3538952 | tf_op jit(solution)/shard_map/ppermute | solution.py:550
  202.8 88.0 %collective-permute-start.22 = (bf16[768,768]{1,0:T(8,128)(2,1)}, bf16[768,768]{1,0:T(8,128)(2,1)}, u32[]{:S(2)}, u32[]{:S(2)}) collective-permute-start(bf16[768,768]{1,0:T(8,128)(2,1)} %collective-permute-done.21.refs_11_), channel_id=1, source_target_pairs={{8,16},{16,24},{9,17},{17,25},{10,18},{18,26},{11,19},{19,27},{12,... | collective-permute-start | bytes 3538952 | tf_op jit(solution)/shard_map/ppermute | solution.py:554
  204.6 60.2 %collective-permute-start.25 = (bf16[960,256]{1,0:T(8,128)(2,1)}, bf16[960,256]{1,0:T(8,128)(2,1)}, u32[]{:S(2)}, u32[]{:S(2)}) collective-permute-start(bf16[960,256]{1,0:T(8,128)(2,1)} %collective-permute-done.24.refs_15_), channel_id=1, source_target_pairs={{8,0},{16,8},{9,1},{17,9},{10,2},{18,10},{11,3},{19,11},{12,4},{20... | collective-permute-start | bytes 1474568 | tf_op jit(solution)/shard_map/ppermute | solution.py:550
  264.8 27.7 %collective-permute-start.28 = (bf16[960,256]{1,0:T(8,128)(2,1)}, bf16[960,256]{1,0:T(8,128)(2,1)}, u32[]{:S(2)}, u32[]{:S(2)}) collective-permute-start(bf16[960,256]{1,0:T(8,128)(2,1)} %collective-permute-done.27.refs_18_), channel_id=1, source_target_pairs={{8,16},{16,24},{9,17},{17,25},{10,18},{18,26},{11,19},{19,27},{12,... | collective-permute-start | bytes 1474568 | tf_op jit(solution)/shard_map/ppermute | solution.py:554
  282.7 116.0 %all-to-all-start.3 = ((bf16[8,112,768]{2,1,0:T(8,128)(2,1)}), bf16[8,112,768]{2,1,0:T(8,128)(2,1)S(1)}, u32[]{:S(2)}, u32[]{:S(2)}) async-start(bf16[8,112,768]{2,1,0:T(8,128)(2,1)} %get-tuple-element.38), calls=%async_computation.3 | async-start | bytes 2752512 | tf_op jit(solution)/shard_map/all_to_all | solution.py:649
  286.5 70.2 %collective-permute-start.14 = (bf16[192,3072]{1,0:T(8,128)(2,1)}, bf16[192,3072]{1,0:T(8,128)(2,1)S(1)}, u32[]{:S(2)}, u32[]{:S(2)}) collective-permute-start(bf16[192,3072]{1,0:T(8,128)(2,1)} %collective-permute-done.13.refs_2_), channel_id=1, source_target_pairs={{8,0},{9,1},{10,2},{11,3},{12,4},{13,5},{14,6},{15,7}} | collective-permute-start | bytes 3538952 | tf_op jit(solution)/shard_map/ppermute | solution.py:550
  287.8 68.9 %collective-permute-start.17 = (bf16[192,3072]{1,0:T(8,128)(2,1)}, bf16[192,3072]{1,0:T(8,128)(2,1)}, u32[]{:S(2)}, u32[]{:S(2)}) collective-permute-start(bf16[192,3072]{1,0:T(8,128)(2,1)} %collective-permute-done.16.refs_5_), channel_id=1, source_target_pairs={{16,24},{17,25},{18,26},{19,27},{20,28},{21,29},{22,30},{23,31}} | collective-permute-start | bytes 3538952 | tf_op jit(solution)/shard_map/ppermute | solution.py:554
  289.5 67.2 %collective-permute-start.20 = (bf16[768,768]{1,0:T(8,128)(2,1)}, bf16[768,768]{1,0:T(8,128)(2,1)}, u32[]{:S(2)}, u32[]{:S(2)}) collective-permute-start(bf16[768,768]{1,0:T(8,128)(2,1)} %collective-permute-done.19.refs_9_), channel_id=1, source_target_pairs={{8,0},{9,1},{10,2},{11,3},{12,4},{13,5},{14,6},{15,7}} | collective-permute-start | bytes 3538952 | tf_op jit(solution)/shard_map/ppermute | solution.py:550
  290.8 65.9 %collective-permute-start.23 = (bf16[768,768]{1,0:T(8,128)(2,1)}, bf16[768,768]{1,0:T(8,128)(2,1)}, u32[]{:S(2)}, u32[]{:S(2)}) collective-permute-start(bf16[768,768]{1,0:T(8,128)(2,1)} %collective-permute-done.22.refs_12_), channel_id=1, source_target_pairs={{16,24},{17,25},{18,26},{19,27},{20,28},{21,29},{22,30},{23,31}} | collective-permute-start | bytes 3538952 | tf_op jit(solution)/shard_map/ppermute | solution.py:554
  292.5 60.2 %collective-permute-start.26 = (bf16[960,256]{1,0:T(8,128)(2,1)}, bf16[960,256]{1,0:T(8,128)(2,1)S(1)}, u32[]{:S(2)}, u32[]{:S(2)}) collective-permute-start(bf16[960,256]{1,0:T(8,128)(2,1)} %collective-permute-done.25.refs_16_), channel_id=1, source_target_pairs={{8,0},{9,1},{10,2},{11,3},{12,4},{13,5},{14,6},{15,7}} | collective-permute-start | bytes 1474568 | tf_op jit(solution)/shard_map/ppermute | solution.py:550
  398.7 46.4 %all-to-all-start.5 = ((bf16[8,112,768]{2,1,0:T(8,128)(2,1)}), bf16[8,112,768]{2,1,0:T(8,128)(2,1)S(1)}, u32[]{:S(2)}, u32[]{:S(2)}) async-start(bf16[8,112,768]{2,1,0:T(8,128)(2,1)} %get-tuple-element.46), calls=%async_computation.5 | async-start | bytes 2752512 | tf_op jit(solution)/shard_map/all_to_all | solution.py:649
  445.1 23.3 %all-to-all-start.6 = ((bf16[8,112,768]{2,1,0:T(8,128)(2,1)}), bf16[8,112,768]{2,1,0:T(8,128)(2,1)}, u32[]{:S(2)}, u32[]{:S(2)}) async-start(bf16[8,112,768]{2,1,0:T(8,128)(2,1)} %get-tuple-element.52), calls=%async_computation.6 | async-start | bytes 2752512 | tf_op jit(solution)/shard_map/all_to_all | solution.py:649
  453.4 21.8 %collective-permute-start.44 = (bf16[192,256]{1,0:T(8,128)(2,1)S(1)}, bf16[192,256]{1,0:T(8,128)(2,1)S(1)}, u32[]{:S(2)}, u32[]{:S(2)}) collective-permute-start(bf16[192,256]{1,0:T(8,128)(2,1)S(1)} %get-tuple-element.109), channel_id=1, source_target_pairs={{24,16},{25,17},{26,18},{27,19},{28,20},{29,21},{30,22},{31,23}} | collective-permute-start | bytes 294920 | tf_op jit(solution)/shard_map/ppermute | solution.py:582
  468.5 79.0 %all-to-all-start.2 = ((bf16[8,112,768]{2,1,0:T(8,128)(2,1)}), bf16[8,112,768]{2,1,0:T(8,128)(2,1)}, u32[]{:S(2)}, u32[]{:S(2)}) async-start(bf16[8,112,768]{2,1,0:T(8,128)(2,1)} %get-tuple-element.36), calls=%async_computation.2 | async-start | bytes 2752512 | tf_op jit(solution)/shard_map/all_to_all | solution.py:649
  477.2 78.1 %collective-permute-start.50 = (bf16[2,128,768]{2,1,0:T(8,128)(2,1)}, bf16[2,128,768]{2,1,0:T(8,128)(2,1)}, u32[]{:S(2)}, u32[]{:S(2)}) collective-permute-start(bf16[2,128,768]{2,1,0:T(8,128)(2,1)} %get-tuple-element.91), channel_id=1, source_target_pairs={{24,16},{25,17},{26,18},{27,19},{28,20},{29,21},{30,22},{31,23}} | collective-permute-start | bytes 1179656 | tf_op jit(solution)/shard_map/ppermute | solution.py:582
  478.6 80.3 %collective-permute-start.43 = (bf16[192,256]{1,0:T(8,128)(2,1)}, bf16[192,256]{1,0:T(8,128)(2,1)}, u32[]{:S(2)}, u32[]{:S(2)}) collective-permute-start(bf16[192,256]{1,0:T(8,128)(2,1)} %get-tuple-element.106), channel_id=1, source_target_pairs={{0,8},{8,16},{16,24},{1,9},{9,17},{17,25},{2,10},{10,18},{18,26},{... | collective-permute-start | bytes 294920 | tf_op jit(solution)/shard_map/ppermute | solution.py:582
  481.8 77.1 %collective-permute-start.46 = (bf16[192,256]{1,0:T(8,128)(2,1)}, bf16[192,256]{1,0:T(8,128)(2,1)}, u32[]{:S(2)}, u32[]{:S(2)}) collective-permute-start(bf16[192,256]{1,0:T(8,128)(2,1)} %fusion.13), channel_id=1, source_target_pairs={{24,16},{16,8},{8,0},{25,17},{17,9},{9,1},{26,18},{18,10},{10,2},{... | collective-permute-start | bytes 294920 | tf_op jit(solution)/shard_map/ppermute | solution.py:582
  485.5 69.8 %collective-permute-start.48 = (bf16[2,128,768]{2,1,0:T(8,128)(2,1)}, bf16[2,128,768]{2,1,0:T(8,128)(2,1)}, u32[]{:S(2)}, u32[]{:S(2)}) collective-permute-start(bf16[2,128,768]{2,1,0:T(8,128)(2,1)} %fusion.7), channel_id=1, source_target_pairs={{0,8},{8,16},{1,9},{9,17},{2,10},{10,18},{3,11},{11,19},{4,12},{12... | collective-permute-start | bytes 1179656 | tf_op jit(solution)/shard_map/ppermute | solution.py:582
  547.5 24.2 %all-to-all-start.4 = ((bf16[8,112,768]{2,1,0:T(8,128)(2,1)}), bf16[8,112,768]{2,1,0:T(8,128)(2,1)}, u32[]{:S(2)}, u32[]{:S(2)}) async-start(bf16[8,112,768]{2,1,0:T(8,128)(2,1)} %get-tuple-element.41), calls=%async_computation.4 | async-start | bytes 2752512 | tf_op jit(solution)/shard_map/all_to_all | solution.py:649
  561.4 46.4 %collective-permute-start.49 = (bf16[2,128,768]{2,1,0:T(8,128)(2,1)}, bf16[2,128,768]{2,1,0:T(8,128)(2,1)S(1)}, u32[]{:S(2)}, u32[]{:S(2)}) collective-permute-start(bf16[2,128,768]{2,1,0:T(8,128)(2,1)} %get-tuple-element.88), channel_id=1, source_target_pairs={{0,8},{8,16},{16,24},{1,9},{9,17},{17,25},{2,10},{10,18},{18,26},{... | collective-permute-start | bytes 1179656 | tf_op jit(solution)/shard_map/ppermute | solution.py:582
  566.3 41.5 %collective-permute-start.52 = (bf16[2,128,768]{2,1,0:T(8,128)(2,1)}, bf16[2,128,768]{2,1,0:T(8,128)(2,1)}, u32[]{:S(2)}, u32[]{:S(2)}) collective-permute-start(bf16[2,128,768]{2,1,0:T(8,128)(2,1)} %fusion.6), channel_id=1, source_target_pairs={{24,16},{16,8},{8,0},{25,17},{17,9},{9,1},{26,18},{18,10},{10,2},{... | collective-permute-start | bytes 1179656 | tf_op jit(solution)/shard_map/ppermute | solution.py:582
  (49 other events, 476.3 us)

commit v2 on v1

--- a/solution.py
+++ b/solution.py
@@ -44,6 +44,10 @@
     first = jnp.mean(scaled, axis=-1, keepdims=True)
     second = jnp.mean(scaled * normal, axis=-1, keepdims=True)
     return inverse * (scaled - first - normal * second)
+
+
+def cost(flops, slowness):
+    return pl.CostEstimate(flops=slowness * flops, bytes_accessed=1 << 20, transcendentals=0)
 
 
 def capacity_of(rows, experts):
@@ -155,16 +159,24 @@
             jax.ShapeDtypeStruct((experts, padded, width), BF16),
         ],
         compiler_params=pltpu.CompilerParams(vmem_limit_bytes=VMEM_LIMIT),
+        cost_estimate=cost(images * length * width * width * 10, 4),
         name="attention_forward",
     )(adapt, x4, side_a, side_b, gains, slots_row)
 
 
 def attention_backward_kernel(
     adapt_ref, count_ref, x_ref, cot_ref, a_ref, b_ref, gains_ref, slots_ref,
-    qkv_ref, weights_ref, mixed_ref, narrow_ref, hidden_ref, home_ref,
-    grad_ref, down_grad_ref, up_grad_ref, grad_qkv_ref, grad_mixed_ref,
+    qkv_ref, weights_ref, mixed_ref, narrow_ref, hidden_ref, home_ref, *refs, add,
 ):
+    refs = list(refs)
+    old_ref = refs.pop(0) if add else None
+    grad_ref, sums_ref, grad_qkv_ref, grad_mixed_ref, acc_ref = refs
     step = pl.program_id(0)
+
+    @pl.when(step == 0)
+    def _():
+        acc_ref[...] = old_ref[...] if add else jnp.zeros_like(acc_ref)
+
     width = x_ref.shape[2]
     heads = width // HEAD_DIM
     x = x_ref[0].astype(F32)
@@ -230,35 +242,22 @@
         down_new = mm_tn(normed, grad_narrow)
         up_new = mm_tn(block, narrow_ref[0, :, part * NARROW : (part + 1) * NARROW])
         cols = slice(part * NARROW, (part + 1) * NARROW)
-
-        @pl.when(step == 0)
-        def _(cols=cols, down_new=down_new, up_new=up_new):
-            down_grad_ref[:, cols] = down_new
-            up_grad_ref[:, cols] = up_new
-
-        @pl.when(step > 0)
-        def _(cols=cols, down_new=down_new, up_new=up_new):
-            down_grad_ref[:, cols] = down_grad_ref[:, cols] + down_new
-            up_grad_ref[:, cols] = up_grad_ref[:, cols] + up_new
-
-    cols = slice(3 * NARROW, 4 * NARROW)
-    down_new = mm_tn(mixed, grad_narrow_out)
-    up_new = mm_tn(branch, narrow_ref[0, :, 3 * NARROW :])
-
-    @pl.when(step == 0)
+        up_cols = slice((4 + part) * NARROW, (5 + part) * NARROW)
+        acc_ref[:, cols] = acc_ref[:, cols] + down_new
+        acc_ref[:, up_cols] = acc_ref[:, up_cols] + up_new
+
+    cols, up_cols = slice(3 * NARROW, 4 * NARROW), slice(7 * NARROW, 8 * NARROW)
+    acc_ref[:, cols] = acc_ref[:, cols] + mm_tn(mixed, grad_narrow_out)
+    acc_ref[:, up_cols] = acc_ref[:, up_cols] + mm_tn(branch, narrow_ref[0, :, 3 * NARROW :])
+
+    @pl.when(step == pl.num_programs(0) - 1)
     def _():
-        down_grad_ref[:, cols] = down_new
-        up_grad_ref[:, cols] = up_new
-
-    @pl.when(step > 0)
-    def _():
-        down_grad_ref[:, cols] = down_grad_ref[:, cols] + down_new
-        up_grad_ref[:, cols] = up_grad_ref[:, cols] + up_new
+        sums_ref[...] = acc_ref[...].astype(sums_ref.dtype)
 
     grad_ref[0] = (grad_hidden + norm_back(grad_normed, normal, inverse, gains_ref[0:1, :])).astype(BF16)
 
 
-def attention_backward(micro, adapt, count, x4, cot4, side_a, side_b, gains, slots_col, kept, home):
+def attention_backward(micro, adapt, count, x4, cot4, side_a, side_b, gains, slots_col, kept, home, old, last):
     qkv, weights, mixed, narrow, hidden = kept
     images = adapt.shape[0]
     _, length, width = x4.shape
@@ -266,8 +265,10 @@
     first = micro * images
     whole = lambda array: pl.BlockSpec(array.shape, lambda i, *_: (0,) * array.ndim)
     image = lambda *dims: pl.BlockSpec((1,) + dims, lambda i, *_: (i,) + (0,) * len(dims))
+    sums = jax.ShapeDtypeStruct((width, 8 * NARROW), BF16 if last else F32)
+    extra = [] if old is None else [old]
     return pl.pallas_call(
-        attention_backward_kernel,
+        functools.partial(attention_backward_kernel, add=old is not None),
         grid_spec=pltpu.PrefetchScalarGridSpec(
             num_scalar_prefetch=2,
             grid=(images,),
@@ -284,22 +285,20 @@
                 image(length, 4 * NARROW),
                 image(length, width),
                 whole(home),
+            ]
+            + [whole(array) for array in extra],
+            out_specs=[image(length, width), whole(sums)],
+            scratch_shapes=[
+                pltpu.VMEM((length, 3 * width), BF16),
+                pltpu.VMEM((length, width), BF16),
+                pltpu.VMEM((width, 8 * NARROW), F32),
             ],
-            out_specs=[
-                image(length, width),
-                pl.BlockSpec((width, 4 * NARROW), lambda i, *_: (0, 0)),
-                pl.BlockSpec((width, 4 * NARROW), lambda i, *_: (0, 0)),
-            ],
-            scratch_shapes=[pltpu.VMEM((length, 3 * width), BF16), pltpu.VMEM((length, width), BF16)],
         ),
-        out_shape=[
-            jax.ShapeDtypeStruct((images, length, width), BF16),
-            jax.ShapeDtypeStruct((width, 4 * NARROW), F32),
-            jax.ShapeDtypeStruct((width, 4 * NARROW), F32),
-        ],
+        out_shape=[jax.ShapeDtypeStruct((images, length, width), BF16), sums],
         compiler_params=pltpu.CompilerParams(vmem_limit_bytes=VMEM_LIMIT),
+        cost_estimate=cost(images * length * width * width * 20, 4),
         name="attention_backward",
-    )(adapt, count, x4, cot4, side_a, side_b, gains, slots_col, qkv, weights, mixed, narrow, hidden, home)
+    )(adapt, count, x4, cot4, side_a, side_b, gains, slots_col, qkv, weights, mixed, narrow, hidden, home, *extra)
 
 
 def dispatch_kernel(count_ref, cot_ref, slots_ref, meta_ref, out_ref):
@@ -391,156 +390,154 @@
 
 
 def expert_kernel(
-    place_ref, rows_ref, arrived_ref, router_ref, *refs, parts, first_call,
+    place_ref, rows_ref, arrived_ref, router_ref, flat_ref, in_ref, out_ref, *refs, first, last, add,
 ):
-    count = 2 * parts - 1
-    ins, outs, smalls = refs[:count], refs[count : 2 * count], refs[2 * count : 3 * count]
-    refs = refs[3 * count :]
-    if not first_call:
-        old_wide_ref, old_tall_ref = refs[:2]
-        refs = refs[2:]
-    (result_ref, sent_ref, wide_ref, tall_ref,
-     in_s, out_s, tall_s, flat_s, sem) = refs
+    refs = list(refs)
+    old_wide_ref = refs.pop(0) if add else None
+    old_tall_ref = refs.pop(0) if add and last else None
+    starts = None if first else (refs.pop(0), refs.pop(0))
+    wide_ref = refs.pop(0)
+    if last:
+        result_ref, sent_ref, tall_ref = refs[:3]
+        refs = refs[3:]
+    forward_ref, backward_ref, left_s, thin_s, turned_s = refs
     step = pl.program_id(0)
-    half, padded, width = rows_ref.shape
-    hidden_units = in_s.shape[1]
-    piece = hidden_units // parts
-    shard = width // parts
-    total = half * padded
-
-    def source(holder, part):
-        return 0 if part == holder else (part - holder if part > holder else parts - 1 + holder - part)
-
-    @pl.when(step == 0)
-    def _():
-        for holder in range(parts):
-            @pl.when(place_ref[0] == holder)
-            def _(holder=holder):
-                copies = []
-                for part in range(parts):
-                    which = source(holder, part)
-                    copies += [
-                        pltpu.make_async_copy(ins[which], in_s.at[pl.ds(part * shard, shard)], sem),
-                        pltpu.make_async_copy(outs[which], out_s.at[pl.ds(part * piece, piece)], sem),
-                        pltpu.make_async_copy(
-                            smalls[which].at[pl.ds(0, piece)], tall_s.at[pl.ds(part * piece, piece)], sem
-                        ),
-                        pltpu.make_async_copy(
-                            smalls[which].at[pl.ds(piece, shard)], flat_s.at[pl.ds(part * shard, shard)], sem
-                        ),
-                    ]
-                for copy in copies:
-                    copy.start()
-                for copy in copies:
-                    copy.wait()
-
-        if first_call:
-            wide_ref[...] = jnp.zeros_like(wide_ref)
-            tall_ref[...] = jnp.zeros_like(tall_ref)
-        else:
-            wide_ref[...] = old_wide_ref[...]
-            tall_ref[...] = old_tall_ref[...]
-
+    experts, padded, width = rows_ref.shape
+    total = experts * padded
+    wider = width + NARROW
     rows = rows_ref[...].reshape(total, width)
     delta = arrived_ref[:, :, :width].reshape(total, width)
     meta = arrived_ref[:, :, width:].reshape(total, LANES).astype(F32)
-    lane = lax.broadcasted_iota(jnp.int32, (total, LANES), 1).astype(F32)
     lane_owner = lane_adapter((total, NARROW)).astype(F32)
     select = jnp.where(jnp.logical_and(lane_owner == meta[:, 0:1], meta[:, 2:3] > 0.5), 1.0, 0.0)
-    own_expert = place_ref[1].astype(F32)
-    is_own = (lane == own_expert).astype(F32)
-    is_other = (lane == meta[:, 1:2]).astype(F32)
-    logits = mm(rows, router_ref[...])
-    own_logit = jnp.sum(logits * is_own, axis=-1, keepdims=True)
-    other_logit = jnp.sum(logits * is_other, axis=-1, keepdims=True)
-    peak = jnp.maximum(own_logit, other_logit)
-    own_exp, other_exp = jnp.exp(own_logit - peak), jnp.exp(other_logit - peak)
-    norm = 1.0 / (own_exp + other_exp)
-    gate, other_gate = own_exp * norm, other_exp * norm
-    grad_result = (delta.astype(F32) * gate).astype(BF16)
-
-    thin_in = (mm(rows, flat_s[:, :NARROW]) * select).astype(BF16)
-    grad_thin_out = (mm(grad_result, flat_s[:, NARROW:]) * select).astype(BF16)
-    result = thin_out = sent = grad_thin_in = None
-    for part in range(parts):
-        cols = slice(part * piece, (part + 1) * piece)
-        in_part = in_s[:, cols]
-        out_part = out_s[cols, :]
-        up_in_t = tall_s[cols, :NARROW]
-        down_out = tall_s[cols, NARROW:]
-        lifted = mm(rows, in_part) + mm_nt(thin_in, up_in_t)
-        value, slope = gelu_pair(lifted)
-        active = value.astype(BF16)
-        grad_active = mm_nt(grad_result, out_part) + mm_nt(grad_thin_out, down_out)
-        grad_lifted = (grad_active * slope).astype(BF16)
-        terms = (mm(active, out_part), mm(active, down_out), mm_nt(grad_lifted, in_part), mm(grad_lifted, up_in_t))
-        if part == 0:
-            result, thin_out, sent, grad_thin_in = terms
+
+    def gates():
+        lane = lax.broadcasted_iota(jnp.int32, (total, LANES), 1).astype(F32)
+        own_expert = place_ref[1].astype(F32)
+        is_own = (lane == own_expert).astype(F32)
+        is_other = (lane == meta[:, 1:2]).astype(F32)
+        logits = mm(rows, router_ref[...])
+        own_logit = jnp.sum(logits * is_own, axis=-1, keepdims=True)
+        other_logit = jnp.sum(logits * is_other, axis=-1, keepdims=True)
+        peak = jnp.maximum(own_logit, other_logit)
+        own_exp, other_exp = jnp.exp(own_logit - peak), jnp.exp(other_logit - peak)
+        norm = 1.0 / (own_exp + other_exp)
+        return own_exp * norm, other_exp * norm, is_own - is_other
+
+    @pl.when(step == 0)
+    def _():
+        gate, _, _ = gates()
+        grad_result = (delta.astype(F32) * gate).astype(BF16)
+        thin_in = mm(rows, flat_ref[:, :NARROW]) * select
+        grad_thin_out = mm(grad_result, flat_ref[:, NARROW:]) * select
+        left_s[:, :width] = grad_result
+        left_s[:, width:] = grad_thin_out.astype(BF16)
+        thin_s[...] = thin_in.astype(BF16)
+        turned_s[:NARROW, :] = thin_in.T.astype(BF16)
+        turned_s[NARROW:, :] = grad_thin_out.T.astype(BF16)
+        if first:
+            forward_ref[...] = jnp.zeros_like(forward_ref)
+            backward_ref[...] = jnp.zeros_like(backward_ref)
         else:
-            result, thin_out, sent, grad_thin_in = (
-                result + terms[0], thin_out + terms[1], sent + terms[2], grad_thin_in + terms[3]
-            )
-        wide_ref[part, 0] = wide_ref[part, 0] + mm_tn(thin_in, grad_lifted)
-        wide_ref[part, 1] = wide_ref[part, 1] + mm_tn(grad_thin_out, active)
-    thin_out = (thin_out * select).astype(BF16)
-    grad_thin_in = (grad_thin_in * select).astype(BF16)
-    result = (result + mm_nt(thin_out, flat_s[:, NARROW:])).astype(BF16).astype(F32)
-    sent = sent + mm_nt(grad_thin_in, flat_s[:, :NARROW])
-    tall_ref[:, :NARROW] = tall_ref[:, :NARROW] + mm_tn(rows, grad_thin_in)
-    tall_ref[:, NARROW:] = tall_ref[:, NARROW:] + mm_tn(grad_result, thin_out)
-    result_ref[...] = (result * gate).astype(BF16).reshape(half, padded, width)
-    grad_gate = jnp.sum(delta.astype(F32) * result, axis=-1, keepdims=True)
-    pull = (is_own - is_other) * (gate * other_gate * grad_gate)
-    high = pull.astype(BF16)
-    rest = (pull - high.astype(F32)).astype(BF16)
-    sent = sent + (mm_nt(high, router_ref[...]) + mm_nt(rest, router_ref[...]))
-    sent_ref[...] = sent.astype(BF16).reshape(half, padded, width)
-
-
-def expert_step(micro, place, rows, arrived, router, pieces, old):
+            forward_ref[...] = starts[0][...]
+            backward_ref[...] = starts[1][...]
+
+    up_in_t = out_ref[:, wider:]
+    lifted = mm(rows, in_ref[...]) + mm_nt(thin_s[...], up_in_t)
+    value, slope = gelu_pair(lifted)
+    active = value.astype(BF16)
+    grad_lifted = (mm_nt(left_s[...], out_ref[:, :wider]) * slope).astype(BF16)
+    forward_ref[...] = forward_ref[...] + mm(active, out_ref[:, :wider])
+    backward_ref[:, :width] = backward_ref[:, :width] + mm_nt(grad_lifted, in_ref[...])
+    backward_ref[:, width:] = backward_ref[:, width:] + mm(grad_lifted, up_in_t)
+    up_new = mm(turned_s[:NARROW, :], grad_lifted)
+    down_new = mm(turned_s[NARROW:, :], active)
+    if add:
+        up_new = up_new + old_wide_ref[0, 0]
+        down_new = down_new + old_wide_ref[0, 1]
+    wide_ref[0, 0] = up_new.astype(wide_ref.dtype)
+    wide_ref[0, 1] = down_new.astype(wide_ref.dtype)
+
+    if last:
+        @pl.when(step == pl.num_programs(0) - 1)
+        def _():
+            gate, other_gate, sides = gates()
+            thin_out = (forward_ref[:, width:] * select).astype(BF16)
+            grad_thin_in = (backward_ref[:, width:] * select).astype(BF16)
+            result = (forward_ref[:, :width] + mm_nt(thin_out, flat_ref[:, NARROW:])).astype(BF16).astype(F32)
+            down_in = mm_tn(grad_thin_in, rows)
+            up_out = mm_tn(thin_out, left_s[:, :width])
+            if add:
+                down_in = down_in + old_tall_ref[:NARROW, :]
+                up_out = up_out + old_tall_ref[NARROW:, :]
+            tall_ref[:NARROW, :] = down_in.astype(tall_ref.dtype)
+            tall_ref[NARROW:, :] = up_out.astype(tall_ref.dtype)
+            result_ref[...] = (result * gate).astype(BF16).reshape(experts, padded, width)
+            grad_gate = jnp.sum(delta.astype(F32) * result, axis=-1, keepdims=True)
+            pull = sides * (gate * other_gate * grad_gate)
+            high = pull.astype(BF16)
+            rest = (pull - high.astype(F32)).astype(BF16)
+            sent = backward_ref[:, :width] + mm_nt(grad_thin_in, flat_ref[:, :NARROW])
+            sent = sent + (mm_nt(high, router_ref[...]) + mm_nt(rest, router_ref[...]))
+            sent_ref[...] = sent.astype(BF16).reshape(experts, padded, width)
+
+
+def expert_step(micro, place, rows, arrived, router, ins, first_ins, outs, parts, starts, last, old):
     experts, padded, width = rows.shape
-    ins, outs, smalls = pieces
-    parts = (len(ins) + 1) // 2
-    hidden_units = ins[0].shape[1]
+    total = experts * padded
+    hidden_units = outs.shape[0]
     piece = hidden_units // parts
-    blocks = 2
-    half = experts // blocks
-    hbm = pl.BlockSpec(memory_space=pl.ANY)
-    wide = jax.ShapeDtypeStruct((parts, 2, NARROW, piece), F32)
-    tall = jax.ShapeDtypeStruct((width, 2 * NARROW), F32)
+    wider = width + NARROW
+    flat_at = (first_ins.shape[1] - 2 * NARROW) // (2 * NARROW)
+    kind = F32 if old is None else BF16
+    wide = jax.ShapeDtypeStruct((parts, 2, NARROW, piece), kind)
+    tall = jax.ShapeDtypeStruct((2 * NARROW, width), kind)
+    sums = jax.ShapeDtypeStruct((total, wider), F32)
     whole = lambda array: pl.BlockSpec(array.shape, lambda i, *_: (0,) * len(array.shape))
-    block = pl.BlockSpec((half, padded, width), lambda i, *_: (i, 0, 0))
-    extra = [] if old is None else list(old)
+    wide_block = pl.BlockSpec((1, 2, NARROW, piece), lambda i, *_: (i, 0, 0, 0))
+    sent = jax.ShapeDtypeStruct((experts, padded, width), BF16)
+    extra, extra_specs = [], []
+    if old is not None:
+        extra.append(old[0])
+        extra_specs.append(wide_block)
+        if last:
+            extra.append(old[1])
+            extra_specs.append(whole(old[1]))
+    if starts is not None:
+        extra += list(starts)
+        extra_specs += [whole(array) for array in starts]
+    if last:
+        out_shape, out_specs = [wide, sent, sent, tall], [wide_block, whole(sent), whole(sent), whole(tall)]
+        scratch = [pltpu.VMEM((total, wider), F32), pltpu.VMEM((total, wider), F32)]
+    else:
+        out_shape, out_specs, scratch = [wide, sums, sums], [wide_block, whole(sums), whole(sums)], []
+    scratch += [
+        pltpu.VMEM((total, wider), BF16),
+        pltpu.VMEM((total, NARROW), BF16),
+        pltpu.VMEM((2 * NARROW, total), BF16),
+    ]
     return pl.pallas_call(
-        functools.partial(expert_kernel, parts=parts, first_call=old is None),
+        functools.partial(expert_kernel, first=starts is None, last=last, add=old is not None),
         grid_spec=pltpu.PrefetchScalarGridSpec(
             num_scalar_prefetch=1,
-            grid=(blocks,),
+            grid=(parts,),
             in_specs=[
-                block,
-                pl.BlockSpec((half, padded, width + LANES), lambda i, *_: (i, micro, 0)),
+                whole(rows),
+                pl.BlockSpec((experts, padded, width + LANES), lambda i, *_: (0, micro, 0)),
                 whole(router),
+                pl.BlockSpec((width, 2 * NARROW), lambda i, *_: (0, flat_at)),
+                pl.BlockSpec((width, piece), lambda i, *_: (0, i)),
+                pl.BlockSpec((piece, wider + NARROW), lambda i, *_: (i, 0)),
             ]
-            + [hbm] * (len(ins) + len(outs) + len(smalls))
-            + [whole(array) for array in extra],
-            out_specs=[block, block, whole(wide), whole(tall)],
-            scratch_shapes=[
-                pltpu.VMEM((width, hidden_units), BF16),
-                pltpu.VMEM((hidden_units, width), BF16),
-                pltpu.VMEM((hidden_units, 2 * NARROW), BF16),
-                pltpu.VMEM((width, 2 * NARROW), BF16),
-                pltpu.SemaphoreType.DMA,
-            ],
+            + extra_specs,
+            out_specs=out_specs,
+            scratch_shapes=scratch,
         ),
-        out_shape=[
-            jax.ShapeDtypeStruct((experts, padded, width), BF16),
-            jax.ShapeDtypeStruct((experts, padded, width), BF16),
-            wide,
-            tall,
-        ],
+        out_shape=out_shape,
         compiler_params=pltpu.CompilerParams(vmem_limit_bytes=VMEM_LIMIT),
+        cost_estimate=cost(8 * total * width * hidden_units, 2),
         name="expert_step",
-    )(place, rows, arrived, router, *ins, *outs, *smalls, *extra)
+    )(place, rows, arrived, router, first_ins, ins, outs, *extra)
 
 
 def line_gather(array, size):
@@ -588,7 +585,7 @@
     return lax.ppermute(array, "expert", [(i, i ^ bit) for i in range(size)])
 
 
-def dense_gather(packed, half, size_dp, size_expert):
+def dense_gather(packed, half, size_dp, size_expert, ahead):
     rows = packed.shape[0]
     if size_expert < 4 or size_expert & (size_expert - 1) or (2 * rows) % 8:
         full = lax.all_gather(packed, ("dp", "expert"), axis=0, tiled=True)
@@ -600,7 +597,7 @@
     other = swap(jnp.where(core == 0, high, low), 1, size_expert)
     pair = jnp.concatenate([jnp.where(core == 0, kept, other), jnp.where(core == 0, other, kept)], axis=0)
     pieces = line_gather(pair, size_dp)
-    stacked = line_stack(pieces, size_dp)
+    stacked, _ = lax.optimization_barrier((line_stack(pieces, size_dp), ahead))
     bits = [1 << b for b in range(1, size_expert.bit_length() - 1)]
     cut = (half // LANES + 1) // 2 * LANES
     done = []
@@ -663,48 +660,28 @@
     padded = -(-capacity // 16) * 16
     shard_rows = attention_in.shape[0]
 
-    half = 2 * width + 4 * NARROW + LANES
-    small = jnp.concatenate([router, norm_gains.T], axis=1)
-    small = jnp.pad(small, ((0, 0), (0, LANES - small.shape[1])))
-    packed = jnp.concatenate(
-        [
-            attention_in[:, : 2 * width],
-            attention_down.reshape(shard_rows, 4 * NARROW),
-            small,
-            attention_in[:, 2 * width :],
-            attention_out,
-            attention_up.reshape(4 * NARROW, shard_rows).T,
-            jnp.zeros((shard_rows, LANES), BF16),
-        ],
-        axis=1,
+    piece, shard = hidden_units // size_dp, width // size_dp
+    chunks = 2 if piece % (2 * LANES) == 0 else 1
+    part = piece // chunks
+    by_shard = expert_in[0].reshape(shard, size_dp, piece)
+    sides = jnp.concatenate(
+        [expert_down_in[0].reshape(shard, NARROW), expert_up_out[0].reshape(NARROW, shard).T], axis=1
     )
-    side_a, side_b = dense_gather(packed, half, size_dp, experts)
-    tail = side_a[:, 2 * width + 4 * NARROW :]
-    gains = tail[:, experts : experts + 2].astype(F32).T
-    router_full = jnp.where(jnp.arange(LANES)[None, :] < experts, tail, jnp.zeros_like(tail))
-
-    own_in = expert_in[0]
-    own_out = expert_out[0]
-    own_small = jnp.concatenate(
-        [
-            jnp.concatenate(
-                [
-                    expert_up_in[0].reshape(NARROW, -1).T,
-                    expert_down_out[0].reshape(-1, NARROW),
-                ],
-                axis=1,
-            ),
-            jnp.concatenate(
-                [
-                    expert_down_in[0].reshape(-1, NARROW),
-                    expert_up_out[0].reshape(NARROW, -1).T,
-                ],
-                axis=1,
-            ),
-        ],
-        axis=0,
+    beside = jnp.concatenate(
+        [expert_out[0], expert_down_out[0].reshape(piece, NARROW), expert_up_in[0].reshape(NARROW, piece).T], axis=1
     )
-    pieces = (line_gather(own_in, size_dp), line_gather(own_out, size_dp), line_gather(own_small, size_dp))
+    weights = []
+    for chunk in range(chunks):
+        own_in = by_shard[:, :, chunk * part : (chunk + 1) * part].reshape(shard, size_dp * part)
+        own_out = beside[chunk * part : (chunk + 1) * part]
+        if chunk == 0:
+            own_in = jnp.concatenate([own_in, sides], axis=1)
+        weights.append(
+            (
+                lax.all_gather(own_in, "dp", axis=0, tiled=True),
+                lax.all_gather(own_out, "dp", axis=0, tiled=True),
+            )
+        )
 
     picks = expert_ids.reshape(micros, 2 * rows)
     hits = (picks[:, :, None] == jnp.arange(experts, dtype=jnp.int32)).astype(jnp.int32)
@@ -723,52 +700,87 @@
     x4 = tokens.reshape(micros * images, length, width)
     cot4 = cotangent.reshape(micros * images, length, width)
     counts = image_count.reshape(micros)
-    arrived = exchange(dispatch(counts, cot4, slots_row, meta, experts, padded))
+    sent_delta = dispatch(counts, cot4, slots_row, meta, experts, padded)
+    arrived = exchange(sent_delta)
+
+    half = 2 * width + 4 * NARROW + LANES
+    small = jnp.concatenate([router, norm_gains.T], axis=1)
+    small = jnp.pad(small, ((0, 0), (0, LANES - small.shape[1])))
+    packed = jnp.concatenate(
+        [
+            attention_in[:, : 2 * width],
+            attention_down.reshape(shard_rows, 4 * NARROW),
+            small,
+            attention_in[:, 2 * width :],
+            attention_out,
+            attention_up.reshape(4 * NARROW, shard_rows).T,
+            jnp.zeros((shard_rows, LANES), BF16),
+        ],
+        axis=1,
+    )
+    side_a, side_b = dense_gather(packed, half, size_dp, experts, sent_delta)
+    tail = side_a[:, 2 * width + 4 * NARROW :]
+    gains = tail[:, experts : experts + 2].astype(F32).T
+    router_full = jnp.where(jnp.arange(LANES)[None, :] < experts, tail, jnp.zeros_like(tail))
 
     place = jnp.stack([lax.axis_index("dp"), lax.axis_index("expert")]).astype(jnp.int32)
     kept, received = [], []
     for micro in range(micros):
-        *saved, sent = attention_forward(
-            micro, adapter_index[micro], x4, side_a, side_b, gains, slots_row, experts, padded
-        )
+        adapt = adapter_index[micro]
+        if kept:
+            adapt, _ = lax.optimization_barrier((adapt, kept[-1][3]))
+        *saved, sent = attention_forward(micro, adapt, x4, side_a, side_b, gains, slots_row, experts, padded)
         kept.append(saved)
         received.append(exchange(sent))
-    old = None
+    step = functools.partial(expert_step, place=place, arrived=arrived, router=router_full, parts=size_dp)
+    sums, old = [None] * micros, [None] * chunks
     results, backs = [], []
+    for chunk in range(chunks):
+        last = chunk == chunks - 1
+        if chunk:
+            step = functools.partial(step, place=lax.optimization_barrier((place, sums[-1][0]))[0])
+        for micro in range(micros):
+            new_wide, *rest = step(
+                micro, rows=received[micro], ins=weights[chunk][0], first_ins=weights[0][0],
+                outs=weights[chunk][1], starts=sums[micro], last=last, old=old[chunk],
+            )
+            old[chunk] = (new_wide, rest[2]) if last else (new_wide, None)
+            if last:
+                results.append(rest[0])
+                back = rest[1]
+                if backs:
+                    back, backs[-1] = lax.optimization_barrier((back, backs[-1]))
+                backs.append(exchange(back))
+            else:
+                sums[micro] = tuple(rest)
+    outputs, input_grads, dense_own = [], [], None
     for micro in range(micros):
-        result, back, *old = expert_step(micro, place, received[micro], arrived, router_full, pieces, old)
-        backs.append(exchange(back))
-        results.append(result)
-    outputs, input_grads, down_total, up_total = [], [], None, None
-    for micro in range(micros):
-        input_grad, down_new, up_new = attention_backward(
+        input_grad, dense_own = attention_backward(
             micro, adapter_index[micro], image_count[micro], x4, cot4, side_a, side_b, gains,
-            slots_col, kept[micro], backs[micro],
+            slots_col, kept[micro], backs[micro], dense_own, micro == micros - 1,
         )
         input_grads.append(input_grad)
-        down_total = down_new if down_total is None else down_total + down_new
-        up_total = up_new if up_total is None else up_total + up_new
+    ahead = backs[-1]
     for micro in range(micros):
-        outputs.append(
-            combine_output(micro, image_count[micro], kept[micro][4], slots_col, exchange(results[micro]))
-        )
-
-    wide, tall = old
-    piece, shard = hidden_units // size_dp, width // size_dp
-    wide = line_scatter(wide.astype(BF16), size_dp)
-    tall = line_scatter(tall.astype(BF16).reshape(size_dp, shard, 2 * NARROW), size_dp)
-    dense = full_scatter(
-        jnp.concatenate([down_total, up_total], axis=1).astype(BF16), size_dp, experts
-    )
+        result, _ = lax.optimization_barrier((results[micro], ahead))
+        ahead = exchange(result)
+        outputs.append(combine_output(micro, image_count[micro], kept[micro][4], slots_col, ahead))
+
+    wide = jnp.concatenate([entry[0] for entry in old], axis=3).reshape(size_dp, 2 * NARROW, piece)
+    tall = jnp.swapaxes(old[-1][1].reshape(2 * NARROW, size_dp, shard), 0, 1)
+    sparse = line_scatter(jnp.concatenate([wide, tall], axis=2).astype(BF16), size_dp)
+    wide = sparse[:, :piece].reshape(2, NARROW, piece)
+    tall = sparse[:, piece:]
+    dense = full_scatter(dense_own.astype(BF16), size_dp, experts)
     return (
         jnp.stack(outputs),
         jnp.stack(input_grads),
         dense[:, : 4 * NARROW].reshape(shard_rows, 4, ADAPTERS, RANK),
         dense[:, 4 * NARROW :].T.reshape(4, ADAPTERS, RANK, shard_rows),
-        tall[:, :NARROW].reshape(1, shard, ADAPTERS, RANK),
+        tall[:NARROW].T.reshape(1, shard, ADAPTERS, RANK),
         wide[0].reshape(1, ADAPTERS, RANK, piece),
         wide[1].T.reshape(1, piece, ADAPTERS, RANK),
-        tall[:, NARROW:].T.reshape(1, ADAPTERS, RANK, shard),
+        tall[NARROW:].reshape(1, ADAPTERS, RANK, shard),
     )
 
 

time: 635 us -> 516 us (0.81)
  waiting for transfers between devices: 220 us -> 122 us
  starting transfers between devices: 134 us -> 78.9 us
  Pallas kernels: 185 us -> 212 us
  between operations: 2.1 us -> 15.2 us
    ppermute x12 -> x3, waiting for transfers between devices: 171 us -> 36.4 us  [line_gather(): lax.ppermute(moving, 'dp', [(i, i - 1) for i in range(1, size - step + 1)])]
    pallas_call x4 -> x6, Pallas kernels: 138 us -> 165 us  [the longest x4 113 us: expert_step(): pl.pallas_call(functools.partial(expert_kernel, first=starts is None, las...]
    ppermute x12 -> x3, starting transfers between devices: 30.4 us -> 6.52 us  [line_gather(): lax.ppermute(moving, 'dp', [(i, i + 1) for i in range(step - 1, size - 1)])]
    ppermute x18 -> x12, starting transfers between devices: 47 us -> 27.4 us  [line_scatter(): arriving = lax.ppermute(message, 'dp', edges)]
    ppermute x11, waiting for transfers between devices: 29.8 us -> 48.6 us  [swap(): return lax.ppermute(array, 'expert', [(i, i ^ bit) for i in range(size)])]
    ppermute x18 -> x12, waiting for transfers between devices: 5.31 us -> 20.3 us  [line_scatter(): arriving = lax.ppermute(message, 'dp', edges)]
    ppermute x12 -> x3, starting transfers between devices: 15.5 us -> 3.84 us  [line_gather(): lax.ppermute(moving, 'dp', [(i, i - 1) for i in range(1, size - step + 1)])]
    all_gather x0 -> x4, waiting for transfers between devices: none -> 10 us  [the longest x2 10 us: shards(): lax.all_gather(own_out, 'dp', axis=0, tiled=True)]
  transfers between devices with their start and end apart: 60 -> 40, of which waited for: 18 -> 15; matrix products, arithmetic and copies ran while one was open for 10% -> 13% of each run, Pallas kernels for 30% -> 35%
where the time goes in v2:
time: 516 us; the launch traced here: 507 us
  Pallas kernels  212 us (41%)
  waiting for transfers between devices  122 us (24%)
  starting transfers between devices  78.9 us (15%)
  local copies, waits for them, and re-layouts  44.2 us (9%)
  other arithmetic  34.6 us (7%)
  between operations  15.2 us (3%)
    pallas_call x4, Pallas kernels, expert_step(): pl.pallas_call(functools.partial(expert_kernel, first=starts is None, las...  113 us
    pallas_call x2, Pallas kernels, attention_backward(): pl.pallas_call(functools.partial(attention_backward_kernel, add=old is no...  52 us
    ppermute x11, waiting for transfers between devices, swap(): return lax.ppermute(array, 'expert', [(i, i ^ bit) for i in range(size)])  48.6 us
    ppermute x3, waiting for transfers between devices, line_gather(): lax.ppermute(moving, 'dp', [(i, i - 1) for i in range(1, size - step + 1)])  36.4 us
    pallas_call x2, Pallas kernels, attention_forward(): pl.pallas_call(attention_forward_kernel, grid_spec=pltpu.PrefetchScalarGr...  33 us
    all_to_all x7, starting transfers between devices, exchange(): lax.all_to_all(array, 'expert', split_axis=0, concat_axis=0, tiled=True)  29 us
    ppermute x12, starting transfers between devices, line_scatter(): arriving = lax.ppermute(message, 'dp', edges)  27.4 us
    ppermute x12, waiting for transfers between devices, line_scatter(): arriving = lax.ppermute(message, 'dp', edges)  20.3 us
  transfers between devices with their start and end apart: 40, of which 15 were waited for; matrix products, arithmetic and copies ran while one was open for 13% of the time, Pallas kernels for 35%

profile of v2, /device:TPU:0, one launch (start us, length us, event | category | flops | bytes accessed | tf_op | source)
XLA Modules:
  0.0 507.2 jit_solution(6641630400899655518)
XLA Ops:
  20.9 5.2 %collective-permute-start.1 = (bf16[48,2176]{1,0:T(8,128)(2,1)}, bf16[48,2176]{1,0:T(8,128)(2,1)}, u32[]{:S(2)}, u32[]{:S(2)}) collective-permute-start(bf16[48,2176]{1,0:T(8,128)(2,1)} %pad_maximum_fusion.11), channel_id=1, source_target_pairs={{0,8},{8,16},{16,24},{1,9},{9,17},{17,25},{2,10},{10,18},{18,26},{... | collective-permute-start | bytes 626696 | tf_op jit(solution)/shard_map/ppermute | solution.py:551
  30.9 4.7 collective-permute-done.1
  36.3 8.6 %collective-permute-done.4 = bf16[48,2176]{1,0:T(8,128)(2,1)} collective-permute-done((bf16[48,2176]{1,0:T(8,128)(2,1)}, bf16[48,2176]{1,0:T(8,128)(2,1)}, u32[]{:S(2)}, u32[]{:S(2)}) %collective-permute-start.4) | collective-permute-done | bytes 208928 | tf_op jit(solution)/shard_map/ppermute | solution.py:547
  46.9 15.7 %collective-permute-done.5 = bf16[48,2176]{1,0:T(8,128)(2,1)S(1)} collective-permute-done((bf16[48,2176]{1,0:T(8,128)(2,1)}, bf16[48,2176]{1,0:T(8,128)(2,1)S(1)}, u32[]{:S(2)}, u32[]{:S(2)}) %collective-permute-start.5) | collective-permute-done | bytes 208928 | tf_op jit(solution)/shard_map/ppermute | solution.py:547
  64.9 6.0 %dispatch.1 = bf16[8,224,896]{2,1,0:T(8,128)(2,1)} custom-call(s32[2]{0:T(128)} %bitcast.224, bf16[4,197,768]{2,1,0:T(8,128)(2,1)} %bitcast.186, s32[4,2,197]{2,1,0:T(2,128)} %copy.114.slots_ref, bf16[4,2,197,128]{3,2,1,0:T(8,128)(2,1)} %select_convert_fusion.meta_ref), custom_call_target="tpu_custom_call" | custom-call | tf_op jit(solution)/shard_map/dispatch/pallas_call | solution.py:327
  70.9 12.1 %collective-permute-done.6 = bf16[48,2176]{1,0:T(8,128)(2,1)S(1)} collective-permute-done((bf16[48,2176]{1,0:T(8,128)(2,1)S(1)}, bf16[48,2176]{1,0:T(8,128)(2,1)S(1)}, u32[]{:S(2)}, u32[]{:S(2)}) %collective-permute-start.6) | collective-permute-done | bytes 208928 | tf_op jit(solution)/shard_map/ppermute | solution.py:547
  87.7 8.1 %collective-permute-done.9 = bf16[4,48,1024]{2,1,0:T(8,128)(2,1)S(1)} collective-permute-done((bf16[4,48,1024]{2,1,0:T(8,128)(2,1)S(1)}, bf16[4,48,1024]{2,1,0:T(8,128)(2,1)S(1)}, u32[]{:S(2)}, u32[]{:S(2)}) %collective-permute-start.9) | collective-permute-done | bytes 393248 | tf_op jit(solution)/shard_map/ppermute | solution.py:585
  102.8 12.3 %collective-permute-done.10 = bf16[4,2,48,1024]{3,2,0,1:T(8,128)(2,1)} collective-permute-done((bf16[4,2,48,1024]{3,2,0,1:T(8,128)(2,1)S(1)}, bf16[4,2,48,1024]{3,2,0,1:T(8,128)(2,1)}, u32[]{:S(2)}, u32[]{:S(2)}) %collective-permute-start.10) | collective-permute-done | bytes 786464 | tf_op jit(solution)/shard_map/ppermute | solution.py:585
  117.3 4.7 collective-permute-done.8
  129.5 4.5 all-to-all-start.1
  138.3 5.0 broadcast_select_fusion
  143.3 5.6 %copy.120.a_ref = bf16[768,2176]{1,0:T(8,128)(2,1)} copy(bf16[768,2176]{0,1:T(8,128)(2,1)} %get-tuple-element.107) | data formatting | bytes 6684672 | tf_op jit(solution)/shard_map/jit(_where)/select_n | solution.py:615
  154.1 16.6 %attention_forward.2 = (bf16[2,197,2304]{2,1,0:T(8,128)(2,1)}, bf16[2,12,197,197]{3,2,1,0:T(8,128)(2,1)}, bf16[2,197,768]{2,1,0:T(8,128)(2,1)}, bf16[2,197,512]{...) custom-call(s32[2]{0:T(128)} %get-tuple-element.148.adapt_ref, bf16[4,197,768]{2,1,0:T(8,128)(2,1)} %bitcast.199, ...), custom_call_target="tpu_custom_call" | custom-call | flops 9295626240 | bytes 1048576 | tf_op jit(solution)/shard_map/attention_forward/pallas_call | solution.py:132
  178.6 16.3 %attention_forward.3 = (bf16[2,197,2304]{2,1,0:T(8,128)(2,1)}, bf16[2,12,197,197]{3,2,1,0:T(8,128)(2,1)}, bf16[2,197,768]{2,1,0:T(8,128)(2,1)}, bf16[2,197,512]{...) custom-call(s32[2]{0:T(128)} %get-tuple-element.48.adapt_ref, bf16[4,197,768]{2,1,0:T(8,128)(2,1)} %bitcast.200, ...), custom_call_target="tpu_custom_call" | custom-call | flops 9295626240 | bytes 1048576 | tf_op jit(solution)/shard_map/attention_forward/pallas_call | solution.py:132
  195.0 4.3 all-to-all-start
  199.4 25.7 %expert_step.4 = (f32[4,2,128,384]{3,2,1,0:T(8,128)}, f32[896,896]{1,0:T(8,128)}, f32[896,896]{1,0:T(8,128)}) custom-call(s32[2]{0:T(128)} %pad_add_fusion.place_ref, bf16[8,112,768]{2,1,0:T(8,128)(2,1)} %copy-done.11, bf16[8,224,896]{2,1,0:T(8,128)(2,1)} %all-to-all-done.1.arrived_ref, bf16[768,128]{1,0:T(8,128)(2,1)} %copy.131.router_ref, ...), custom_call_target="tpu_custom_call" | custom-call | flops 16911433728 | bytes 1048576 | tf_op jit(solution)/shard_map/expert_step/pallas_call | solution.py:519
  226.2 25.7 %expert_step.5 = (bf16[4,2,128,384]{3,2,1,0:T(8,128)(2,1)}, f32[896,896]{1,0:T(8,128)}, f32[896,896]{1,0:T(8,128)}) custom-call(s32[2]{0:T(128)} %pad_add_fusion.place_ref, bf16[8,112,768]{2,1,0:T(8,128)(2,1)} %copy-done.12, bf16[8,224,896]{2,1,0:T(8,128)(2,1)} %all-to-all-done.1.arrived_ref, bf16[768,128]{1,0:T(8,128)(2,1)} %copy.131.router_ref, ...), custom_call_target="tpu_custom_call" | custom-call | flops 16911433728 | bytes 1048576 | tf_op jit(solution)/shard_map/expert_step/pallas_call | solution.py:519
  251.9 10.0 %all-gather.11.cloned.1.call-done.out_ref = bf16[1536,1024]{1,0:T(8,128)(2,1)} async-done(((bf16[384,1024]{1,0:T(8,128)(2,1)}), bf16[1536,1024]{1,0:T(8,128)(2,1)}) %all-gather.11.cloned.1.call-update) | async-done | bytes 3145744 | tf_op jit(solution)/shard_map/all_gather | solution.py:682
  261.9 30.8 %expert_step.6 = (f32[4,2,128,384]{3,2,1,0:T(8,128)}, bf16[8,112,768]{2,1,0:T(8,128)(2,1)}, bf16[8,112,768]{2,1,0:T(8,128)(2,1)}, f32[256,768]{1,0:T(8,128)}) custom-call(s32[2]{0:T(128)} %pad_add_fusion.place_ref, bf16[8,112,768]{2,1,0:T(8,128)(2,1)} %copy-done.11, bf16[8,224,896]{2,1,0:T(8,128)(2,1)} %all-to-all-done.1.arrived_ref, ...), custom_call_target="tpu_custom_call" | custom-call | flops 16911433728 | bytes 1048576 | tf_op jit(solution)/shard_map/expert_step/pallas_call | solution.py:519
  296.6 30.5 %expert_step.7 = (bf16[4,2,128,384]{3,2,1,0:T(8,128)(2,1)}, bf16[8,112,768]{2,1,0:T(8,128)(2,1)}, bf16[8,112,768]{2,1,0:T(8,128)(2,1)}, bf16[256,768]{1,0:T(8,128)(2,1)}) custom-call(s32[2]{0:T(128)} %pad_add_fusion.place_ref, bf16[8,112,768]{2,1,0:T(8,128)(2,1)} %copy-done.12, bf16[8,224,896]{2,1,0:T(8,128)(2,1)} %all-to-all-done.1.arrived_ref, ...), custom_call_target="tpu_custom_call" | custom-call | flops 16911433728 | bytes 1048576 | tf_op jit(solution)/shard_map/expert_step/pallas_call | solution.py:519
  334.7 4.5 all-to-all-start.4
  339.2 25.7 %attention_backward.2 = (bf16[2,197,768]{2,1,0:T(8,128)(2,1)}, f32[768,1024]{1,0:T(8,128)}) custom-call(s32[2]{0:T(128)} %get-tuple-element.148.adapt_ref, s32[1]{0:T(128)} %bitcast.count_ref, bf16[4,197,768]{2,1,0:T(8,128)(2,1)} %bitcast.201, bf16[4,197,768]{2,1,0:T(8,128)(2,1)} %bitcast.187, bf16[768,2176]{1,0:T(8,128)(2,1)} %copy.120.a_ref, ...), custom_call_target="tpu_custom_call" | custom-call | flops 18591252480 | bytes 1048576 | tf_op jit(solution)/shard_map/attention_backward/pallas_call | solution.py:270
  364.9 26.3 %attention_backward.3 = (bf16[2,197,768]{2,1,0:T(8,128)(2,1)}, bf16[768,1024]{1,0:T(8,128)(2,1)}) custom-call(s32[2]{0:T(128)} %get-tuple-element.48.adapt_ref, s32[1]{0:T(128)} %bitcast.44.count_ref, bf16[4,197,768]{2,1,0:T(8,128)(2,1)} %bitcast.202, bf16[4,197,768]{2,1,0:T(8,128)(2,1)} %bitcast.188, bf16[768,2176]{1,0:T(8,128)(2,1)} %copy.120.a_ref, ...), custom_call_target="tpu_custom_call" | custom-call | flops 18591252480 | bytes 1048576 | tf_op jit(solution)/shard_map/attention_backward/pallas_call | solution.py:270
  399.1 10.5 %collective-permute-done.24 = bf16[256,960]{1,0:T(8,128)(2,1)S(1)} collective-permute-done((bf16[256,960]{1,0:T(8,128)(2,1)}, bf16[256,960]{1,0:T(8,128)(2,1)S(1)}, u32[]{:S(2)}, u32[]{:S(2)}) %collective-permute-start.24) | collective-permute-done | bytes 491552 | tf_op jit(solution)/shard_map/ppermute | solution.py:579
  410.9 7.2 %collective-permute-start.25 = (bf16[256,960]{1,0:T(8,128)(2,1)S(1)}, bf16[256,960]{1,0:T(8,128)(2,1)S(1)}, u32[]{:S(2)}, u32[]{:S(2)}) collective-permute-start(bf16[256,960]{1,0:T(8,128)(2,1)S(1)} %get-tuple-element.108), channel_id=1, source_target_pairs={{0,8},{8,16},{16,24},{1,9},{9,17},{17,25},{2,10},{10,18},{18,26},{... | collective-permute-start | bytes 1474568 | tf_op jit(solution)/shard_map/ppermute | solution.py:579
  422.7 5.7 %collective-permute-done.25 = bf16[256,960]{1,0:T(8,128)(2,1)S(1)} collective-permute-done((bf16[256,960]{1,0:T(8,128)(2,1)S(1)}, bf16[256,960]{1,0:T(8,128)(2,1)S(1)}, u32[]{:S(2)}, u32[]{:S(2)}) %collective-permute-start.25) | collective-permute-done | bytes 491552 | tf_op jit(solution)/shard_map/ppermute | solution.py:579
  428.4 4.1 collective-permute-done.28
  432.8 4.7 all-to-all-start.5
  440.7 19.5 %collective-permute-done.13 = bf16[4,2,24,512]{3,2,0,1:T(8,128)(2,1)S(1)} collective-permute-done((bf16[4,2,24,512]{3,2,0,1:T(8,128)(2,1)S(1)}, bf16[4,2,24,512]{3,2,0,1:T(8,128)(2,1)S(1)}, u32[]{:S(2)}, u32[]{:S(2)}) %collective-permute-start.13) | collective-permute-done | bytes 196640 | tf_op jit(solution)/shard_map/ppermute | solution.py:585
  476.7 5.9 %collective-permute-start.19 = (bf16[24,1024]{1,0:T(8,128)(2,1)S(1)}, bf16[24,1024]{1,0:T(8,128)(2,1)S(1)}, u32[]{:S(2)}, u32[]{:S(2)}) collective-permute-start(bf16[24,1024]{1,0:T(8,128)(2,1)S(1)} %get-tuple-element.140), channel_id=1, source_target_pairs={{0,8},{8,16},{16,24},{1,9},{9,17},{17,25},{2,10},{10,18},{18,26},{... | collective-permute-start | bytes 147464 | tf_op jit(solution)/shard_map/ppermute | solution.py:579
  486.0 4.1 combine_output.2
  493.0 4.1 combine_output.3
  (229 shorter events, 117.2 us)
Async XLA Ops:
  7.2 192.2 %all-gather.5.cloned.1.call-start = ((), (), s32[]{:S(2)}) async-start(), calls=%async_computation.7 | async-start | bytes 3440640 | tf_op jit(solution)/shard_map/all_gather | solution.py:681
  11.9 187.4 %all-gather.7.cloned.1.call-start = ((), (), s32[]{:S(2)}) async-start(), calls=%async_computation.8 | async-start | bytes 3932160 | tf_op jit(solution)/shard_map/all_gather | solution.py:682
  15.0 236.9 %all-gather.9.cloned.1.call-start = ((), (), s32[]{:S(2)}) async-start(), calls=%async_computation.9 | async-start | bytes 2949120 | tf_op jit(solution)/shard_map/all_gather | solution.py:681
  20.9 14.7 %collective-permute-start.1 = (bf16[48,2176]{1,0:T(8,128)(2,1)}, bf16[48,2176]{1,0:T(8,128)(2,1)}, u32[]{:S(2)}, u32[]{:S(2)}) collective-permute-start(bf16[48,2176]{1,0:T(8,128)(2,1)} %pad_maximum_fusion.11), channel_id=1, source_target_pairs={{0,8},{8,16},{16,24},{1,9},{9,17},{17,25},{2,10},{10,18},{18,26},{... | collective-permute-start | bytes 626696 | tf_op jit(solution)/shard_map/ppermute | solution.py:551
  26.1 18.8 %collective-permute-start.4 = (bf16[48,2176]{1,0:T(8,128)(2,1)}, bf16[48,2176]{1,0:T(8,128)(2,1)}, u32[]{:S(2)}, u32[]{:S(2)}) collective-permute-start(bf16[48,2176]{1,0:T(8,128)(2,1)} %pad_maximum_fusion.11), channel_id=1, source_target_pairs={{8,0},{16,8},{24,16},{9,1},{17,9},{25,17},{10,2},{18,10},{26,18},{... | collective-permute-start | bytes 626696 | tf_op jit(solution)/shard_map/ppermute | solution.py:547
  35.6 10.6 %collective-permute-start.2 = (bf16[48,2176]{1,0:T(8,128)(2,1)}, bf16[48,2176]{1,0:T(8,128)(2,1)S(1)}, u32[]{:S(2)}, u32[]{:S(2)}) collective-permute-start(bf16[48,2176]{1,0:T(8,128)(2,1)} %collective-permute-done.1), channel_id=1, source_target_pairs={{8,16},{16,24},{9,17},{17,25},{10,18},{18,26},{11,19},{19,27},{12,... | collective-permute-start | bytes 626696 | tf_op jit(solution)/shard_map/ppermute | solution.py:551
  44.9 17.7 %collective-permute-start.5 = (bf16[48,2176]{1,0:T(8,128)(2,1)}, bf16[48,2176]{1,0:T(8,128)(2,1)S(1)}, u32[]{:S(2)}, u32[]{:S(2)}) collective-permute-start(bf16[48,2176]{1,0:T(8,128)(2,1)} %collective-permute-done.4), channel_id=1, source_target_pairs={{8,0},{16,8},{9,1},{17,9},{10,2},{18,10},{11,3},{19,11},{12,4},{20... | collective-permute-start | bytes 626696 | tf_op jit(solution)/shard_map/ppermute | solution.py:547
  46.2 24.7 %collective-permute-start.3 = (bf16[48,2176]{1,0:T(8,128)(2,1)S(1)}, bf16[48,2176]{1,0:T(8,128)(2,1)S(1)}, u32[]{:S(2)}, u32[]{:S(2)}) collective-permute-start(bf16[48,2176]{1,0:T(8,128)(2,1)S(1)} %collective-permute-done.2), channel_id=1, source_target_pairs={{16,24},{17,25},{18,26},{19,27},{20,28},{21,29},{22,30},{23,31}} | collective-permute-start | bytes 626696 | tf_op jit(solution)/shard_map/ppermute | solution.py:551
  62.6 20.5 %collective-permute-start.6 = (bf16[48,2176]{1,0:T(8,128)(2,1)S(1)}, bf16[48,2176]{1,0:T(8,128)(2,1)S(1)}, u32[]{:S(2)}, u32[]{:S(2)}) collective-permute-start(bf16[48,2176]{1,0:T(8,128)(2,1)S(1)} %collective-permute-done.5), channel_id=1, source_target_pairs={{8,0},{9,1},{10,2},{11,3},{12,4},{13,5},{14,6},{15,7}} | collective-permute-start | bytes 626696 | tf_op jit(solution)/shard_map/ppermute | solution.py:547
  84.6 11.2 %collective-permute-start.9 = (bf16[4,48,1024]{2,1,0:T(8,128)(2,1)S(1)}, bf16[4,48,1024]{2,1,0:T(8,128)(2,1)S(1)}, u32[]{:S(2)}, u32[]{:S(2)}) collective-permute-start(bf16[4,48,1024]{2,1,0:T(8,128)(2,1)S(1)} %slice.100), channel_id=1, source_target_pairs={{0,4},{1,5},{2,6},{3,7},{4,0},{5,1},{6,2},{7,3},{8,12},{9,13},{10,... | collective-permute-start | bytes 1179656 | tf_op jit(solution)/shard_map/ppermute | solution.py:585
  86.1 12.3 %collective-permute-start.7 = (bf16[4,48,1152]{2,1,0:T(8,128)(2,1)S(1)}, bf16[4,48,1152]{2,1,0:T(8,128)(2,1)}, u32[]{:S(2)}, u32[]{:S(2)}) collective-permute-start(bf16[4,48,1152]{2,1,0:T(8,128)(2,1)S(1)} %slice.99), channel_id=1, source_target_pairs={{0,2},{1,3},{2,0},{3,1},{4,6},{5,7},{6,4},{7,5},{8,10},{9,11},{10,... | collective-permute-start | bytes 1327112 | tf_op jit(solution)/shard_map/ppermute | solution.py:585
  95.9 19.2 %collective-permute-start.10 = (bf16[4,2,48,1024]{3,2,0,1:T(8,128)(2,1)S(1)}, bf16[4,2,48,1024]{3,2,0,1:T(8,128)(2,1)}, u32[]{:S(2)}, u32[]{:S(2)}) collective-permute-start(bf16[4,2,48,1024]{3,2,0,1:T(8,128)(2,1)S(1)} %pad_maximum_fusion.9), channel_id=1, source_target_pairs={{0,2},{1,3},{2,0},{3,1},{4,6},{5,7},{6,4},{7,5},{8,10},{9,11},{10,... | collective-permute-start | bytes 2359304 | tf_op jit(solution)/shard_map/ppermute | solution.py:585
  101.3 20.7 %collective-permute-start.8 = (bf16[4,2,48,1152]{3,2,1,0:T(8,128)(2,1)}, bf16[4,2,48,1152]{3,2,1,0:T(8,128)(2,1)}, u32[]{:S(2)}, u32[]{:S(2)}) collective-permute-start(bf16[4,2,48,1152]{3,2,1,0:T(8,128)(2,1)} %pad_maximum_fusion.7), channel_id=1, source_target_pairs={{0,4},{1,5},{2,6},{3,7},{4,0},{5,1},{6,2},{7,3},{8,12},{9,13},{10,... | collective-permute-start | bytes 2654216 | tf_op jit(solution)/shard_map/ppermute | solution.py:585
  129.5 43.0 %all-to-all-start.1 = ((bf16[8,224,896]{2,1,0:T(8,128)(2,1)}), bf16[8,224,896]{2,1,0:T(8,128)(2,1)}, u32[]{:S(2)}, u32[]{:S(2)}) async-start(bf16[8,224,896]{2,1,0:T(8,128)(2,1)} %dispatch.1), calls=%async_computation.1 | async-start | bytes 6422528 | tf_op jit(solution)/shard_map/all_to_all | solution.py:646
  134.0 127.9 %all-gather.11.cloned.1.call-start = ((), (), s32[]{:S(2)}) async-start(), calls=%async_computation.10 | async-start | bytes 3932160 | tf_op jit(solution)/shard_map/all_gather | solution.py:682
  172.6 22.4 %all-to-all-start.2 = ((bf16[8,112,768]{2,1,0:T(8,128)(2,1)}), bf16[8,112,768]{2,1,0:T(8,128)(2,1)S(1)}, u32[]{:S(2)}, u32[]{:S(2)}) async-start(bf16[8,112,768]{2,1,0:T(8,128)(2,1)} %get-tuple-element.50), calls=%async_computation.2 | async-start | bytes 2752512 | tf_op jit(solution)/shard_map/all_to_all | solution.py:646
  195.0 30.1 %all-to-all-start = ((bf16[8,112,768]{2,1,0:T(8,128)(2,1)}), bf16[8,112,768]{2,1,0:T(8,128)(2,1)S(1)}, u32[]{:S(2)}, u32[]{:S(2)}) async-start(bf16[8,112,768]{2,1,0:T(8,128)(2,1)} %get-tuple-element.49), calls=%async_computation | async-start | bytes 2752512 | tf_op jit(solution)/shard_map/all_to_all | solution.py:646
  292.7 42.0 %all-to-all-start.3 = ((bf16[8,112,768]{2,1,0:T(8,128)(2,1)}), bf16[8,112,768]{2,1,0:T(8,128)(2,1)S(1)}, u32[]{:S(2)}, u32[]{:S(2)}) async-start(bf16[8,112,768]{2,1,0:T(8,128)(2,1)} %get-tuple-element.61), calls=%async_computation.3 | async-start | bytes 2752512 | tf_op jit(solution)/shard_map/all_to_all | solution.py:646
  331.1 62.7 %collective-permute-start.23 = (bf16[256,960]{1,0:T(8,128)(2,1)}, bf16[256,960]{1,0:T(8,128)(2,1)}, u32[]{:S(2)}, u32[]{:S(2)}) collective-permute-start(bf16[256,960]{1,0:T(8,128)(2,1)} %get-tuple-element.112), channel_id=1, source_target_pairs={{0,8},{1,9},{2,10},{3,11},{4,12},{5,13},{6,14},{7,15}} | collective-permute-start | bytes 1474568 | tf_op jit(solution)/shard_map/ppermute | solution.py:579
  333.2 60.6 %collective-permute-start.26 = (bf16[256,960]{1,0:T(8,128)(2,1)}, bf16[256,960]{1,0:T(8,128)(2,1)}, u32[]{:S(2)}, u32[]{:S(2)}) collective-permute-start(bf16[256,960]{1,0:T(8,128)(2,1)} %get-tuple-element.113), channel_id=1, source_target_pairs={{24,16},{25,17},{26,18},{27,19},{28,20},{29,21},{30,22},{31,23}} | collective-permute-start | bytes 1474568 | tf_op jit(solution)/shard_map/ppermute | solution.py:579
  334.7 30.2 %all-to-all-start.4 = ((bf16[8,112,768]{2,1,0:T(8,128)(2,1)}), bf16[8,112,768]{2,1,0:T(8,128)(2,1)}, u32[]{:S(2)}, u32[]{:S(2)}) async-start(bf16[8,112,768]{2,1,0:T(8,128)(2,1)} %get-tuple-element.62), calls=%async_computation.4 | async-start | bytes 2752512 | tf_op jit(solution)/shard_map/all_to_all | solution.py:646
  393.3 26.2 %collective-permute-start.12 = (bf16[4,2,2,24,1024]{4,3,2,1,0:T(8,128)(2,1)}, bf16[4,2,2,24,1024]{4,3,2,1,0:T(8,128)(2,1)S(1)}, u32[]{:S(2)}, u32[]{:S(2)}) collective-permute-start(bf16[4,2,2,24,1024]{4,3,2,1,0:T(8,128)(2,1)} %dynamic-slice_bitcast_fusion), channel_id=1, source_target_pairs={{0,1},{1,0},{2,3},{3,2},{4,5},{5,4},{6,7},{7,6},{8,9},{9,8},{10,11... | collective-permute-start | bytes 2359304 | tf_op jit(solution)/shard_map/ppermute | solution.py:585
  396.3 13.2 %collective-permute-start.24 = (bf16[256,960]{1,0:T(8,128)(2,1)}, bf16[256,960]{1,0:T(8,128)(2,1)S(1)}, u32[]{:S(2)}, u32[]{:S(2)}) collective-permute-start(bf16[256,960]{1,0:T(8,128)(2,1)} %get-tuple-element.110), channel_id=1, source_target_pairs={{0,8},{8,16},{1,9},{9,17},{2,10},{10,18},{3,11},{11,19},{4,12},{12... | collective-permute-start | bytes 1474568 | tf_op jit(solution)/shard_map/ppermute | solution.py:579
  397.7 11.9 %collective-permute-start.27 = (bf16[256,960]{1,0:T(8,128)(2,1)}, bf16[256,960]{1,0:T(8,128)(2,1)}, u32[]{:S(2)}, u32[]{:S(2)}) collective-permute-start(bf16[256,960]{1,0:T(8,128)(2,1)} %get-tuple-element.111), channel_id=1, source_target_pairs={{24,16},{16,8},{25,17},{17,9},{26,18},{18,10},{27,19},{19,11},{28,... | collective-permute-start | bytes 1474568 | tf_op jit(solution)/shard_map/ppermute | solution.py:579
  410.9 17.4 %collective-permute-start.25 = (bf16[256,960]{1,0:T(8,128)(2,1)S(1)}, bf16[256,960]{1,0:T(8,128)(2,1)S(1)}, u32[]{:S(2)}, u32[]{:S(2)}) collective-permute-start(bf16[256,960]{1,0:T(8,128)(2,1)S(1)} %get-tuple-element.108), channel_id=1, source_target_pairs={{0,8},{8,16},{16,24},{1,9},{9,17},{17,25},{2,10},{10,18},{18,26},{... | collective-permute-start | bytes 1474568 | tf_op jit(solution)/shard_map/ppermute | solution.py:579
  418.2 14.3 %collective-permute-start.28 = (bf16[256,960]{1,0:T(8,128)(2,1)S(1)}, bf16[256,960]{1,0:T(8,128)(2,1)S(1)}, u32[]{:S(2)}, u32[]{:S(2)}) collective-permute-start(bf16[256,960]{1,0:T(8,128)(2,1)S(1)} %get-tuple-element.109), channel_id=1, source_target_pairs={{24,16},{16,8},{8,0},{25,17},{17,9},{9,1},{26,18},{18,10},{10,2},{... | collective-permute-start | bytes 1474568 | tf_op jit(solution)/shard_map/ppermute | solution.py:579
  420.7 18.9 %collective-permute-start.15 = (bf16[4,2,24,512]{3,2,1,0:T(8,128)(2,1)}, bf16[4,2,24,512]{3,2,1,0:T(8,128)(2,1)}, u32[]{:S(2)}, u32[]{:S(2)}) collective-permute-start(bf16[4,2,24,512]{3,2,1,0:T(8,128)(2,1)} %dynamic-slice_bitcast_fusion.1), channel_id=1, source_target_pairs={{0,4},{1,5},{2,6},{3,7},{4,0},{5,1},{6,2},{7,3},{8,12},{9,13},{10,... | collective-permute-start | bytes 589832 | tf_op jit(solution)/shard_map/ppermute | solution.py:585
  432.8 36.4 %all-to-all-start.5 = ((bf16[8,112,768]{2,1,0:T(8,128)(2,1)}), bf16[8,112,768]{2,1,0:T(8,128)(2,1)S(1)}, u32[]{:S(2)}, u32[]{:S(2)}) async-start(bf16[8,112,768]{2,1,0:T(8,128)(2,1)} %get-tuple-element.63), calls=%async_computation.5 | async-start | bytes 2752512 | tf_op jit(solution)/shard_map/all_to_all | solution.py:646
  437.5 22.7 %collective-permute-start.13 = (bf16[4,2,24,512]{3,2,0,1:T(8,128)(2,1)S(1)}, bf16[4,2,24,512]{3,2,0,1:T(8,128)(2,1)S(1)}, u32[]{:S(2)}, u32[]{:S(2)}) collective-permute-start(bf16[4,2,24,512]{3,2,0,1:T(8,128)(2,1)S(1)} %bitcast.216), channel_id=1, source_target_pairs={{0,2},{1,3},{2,0},{3,1},{4,6},{5,7},{6,4},{7,5},{8,10},{9,11},{10,... | collective-permute-start | bytes 589832 | tf_op jit(solution)/shard_map/ppermute | solution.py:585
  440.6 21.2 %collective-permute-start.16 = (bf16[4,24,512]{2,1,0:T(8,128)(2,1)S(1)}, bf16[4,24,512]{2,1,0:T(8,128)(2,1)S(1)}, u32[]{:S(2)}, u32[]{:S(2)}) collective-permute-start(bf16[4,24,512]{2,1,0:T(8,128)(2,1)S(1)} %dynamic-slice_bitcast_fusion.2), channel_id=1, source_target_pairs={{0,2},{1,3},{2,0},{3,1},{4,6},{5,7},{6,4},{7,5},{8,10},{9,11},{10,... | collective-permute-start | bytes 294920 | tf_op jit(solution)/shard_map/ppermute | solution.py:585
  469.2 22.7 %all-to-all-start.6 = ((bf16[8,112,768]{2,1,0:T(8,128)(2,1)}), bf16[8,112,768]{2,1,0:T(8,128)(2,1)S(1)}, u32[]{:S(2)}, u32[]{:S(2)}) async-start(bf16[8,112,768]{2,1,0:T(8,128)(2,1)} %get-tuple-element.66), calls=%async_computation.6 | async-start | bytes 2752512 | tf_op jit(solution)/shard_map/all_to_all | solution.py:646
  476.7 13.4 %collective-permute-start.19 = (bf16[24,1024]{1,0:T(8,128)(2,1)S(1)}, bf16[24,1024]{1,0:T(8,128)(2,1)S(1)}, u32[]{:S(2)}, u32[]{:S(2)}) collective-permute-start(bf16[24,1024]{1,0:T(8,128)(2,1)S(1)} %get-tuple-element.140), channel_id=1, source_target_pairs={{0,8},{8,16},{16,24},{1,9},{9,17},{17,25},{2,10},{10,18},{18,26},{... | collective-permute-start | bytes 147464 | tf_op jit(solution)/shard_map/ppermute | solution.py:579
  (39 other events, 220.0 us)
Sparse Core Ops, SparseCore 0:
  12.1 68.3 all-gather.4
  82.0 65.3 all-gather.6
  149.0 48.6 all-gather.8
  199.7 62.1 all-gather.10
